TPU v7x, 128 devices: a whole 4x4x4 slice. The times are simulated.
128 devices in a mesh: section: 8 (over z, y_lo), tensor: 16 (over x, y_hi, core).
Axes of the slice: x: 4, y: 4 (y_hi: 2, y_lo: 2; y = y_hi * 2 + y_lo), z: 4, core: 2. Of those that a mesh axis runs over, the one named last changes fastest.
Arguments:
- tokens: bfloat16 [384, 6144], P('tensor', 'section'), may hold values from -6 to 6
- combine: float32 [384, 2], replicated, may hold values from 0.1 to 1
- expert_ids: int32 [384, 2], replicated, may hold values from 0 to 3, as said below
- expert_counts: int32 [4], replicated, may hold values from 0 to 384, as said below
- w_gate: bfloat16 [4, 6144, 16384], P(None, 'section', 'tensor'), may hold values from -0.078125 to 0.078125
- w_up: bfloat16 [4, 6144, 16384], P(None, 'section', 'tensor'), may hold values from -0.078125 to 0.078125
- w_down: bfloat16 [4, 16384, 6144], P(None, 'tensor', 'section'), may hold values from -0.046875 to 0.046875
- cotangent: bfloat16 [384, 6144], P('tensor', 'section'), may hold values from -6 to 6
Outputs:
- layer_out: bfloat16 [384, 6144], P('tensor', 'section')
- d_tokens: bfloat16 [384, 6144], P('tensor', 'section')
- d_down: bfloat16 [4, 16384, 6144], P(None, 'tensor', 'section')
Inputs may be any that keep to these rules, and one draw needn't show every extreme that they name: `expert_ids`: each row names two different experts; one expert, drawn from the seed, is named by every row. expert_counts[e] is the number of entries of expert_ids equal to e.
All inputs are finite; a program needn't handle non-finite values.
Results may differ from a plain program's by a relative error of at most 0.0058.
Values may be sent and summed in bfloat16 or wider, within the bound.
A program may use at most 128 MiB of HBM per device.

v0:
```python
import jax
import jax.numpy as jnp
from jax import lax
from jax.sharding import PartitionSpec as P

EXPERTS = 4
BLOCK = 128


def route_layout(expert_ids, expert_counts, tokens_total, capacity):
    flat_ids = expert_ids.reshape(-1)
    onehot = (flat_ids[:, None] == jnp.arange(EXPERTS, dtype=jnp.int32)[None, :]).astype(jnp.int32)
    within = jnp.sum((jnp.cumsum(onehot, 0) - onehot) * onehot, 1)
    padded = (expert_counts + BLOCK - 1) // BLOCK * BLOCK
    block_ends = jnp.cumsum(padded)
    block_starts = block_ends - padded
    slot_index = jnp.sum(onehot * block_starts[None, :], 1) + within
    entry_token = jnp.arange(flat_ids.shape[0], dtype=jnp.int32) // 2
    owner_token = jnp.full((capacity,), tokens_total, jnp.int32).at[slot_index].set(entry_token)
    first_rows = jnp.arange(capacity // BLOCK, dtype=jnp.int32) * BLOCK
    block_expert = jnp.minimum(
        jnp.sum((block_ends[None, :] <= first_rows[:, None]).astype(jnp.int32), 1), EXPERTS - 1
    )
    return (slot_index, owner_token, block_expert)


def blocked_product(rows, weights, block_expert, transpose):
    nblocks = block_expert.shape[0]
    blocks = rows.reshape(nblocks, rows.shape[0] // nblocks, rows.shape[1])

    def apply_block(operand):
        segment, expert = operand
        matrix = lax.dynamic_index_in_dim(weights, expert, 0, keepdims=False)
        if transpose:
            return lax.dot_general(
                segment, matrix, (((1,), (1,)), ((), ())), preferred_element_type=jnp.float32
            )
        return jnp.dot(segment, matrix, preferred_element_type=jnp.float32)

    result = lax.map(apply_block, (blocks, block_expert))
    return result.reshape(rows.shape[0], result.shape[2])


def gate_forward(gate, up):
    sigmoid = jax.nn.sigmoid(gate)
    return (gate * sigmoid * up).astype(jnp.bfloat16)


def gate_backward(d_hidden, gate, up):
    sigmoid = jax.nn.sigmoid(gate)
    d_gate = (d_hidden * up * sigmoid * (1.0 + gate * (1.0 - sigmoid))).astype(jnp.bfloat16)
    d_up = (d_hidden * gate * sigmoid).astype(jnp.bfloat16)
    return (d_gate, d_up)


def on_device(tokens, combine, expert_ids, expert_counts, w_gate, w_up, w_down, cotangent):
    tokens_total = combine.shape[0]
    capacity = 2 * tokens_total + EXPERTS * BLOCK
    slot_index, owner_token, block_expert = route_layout(
        expert_ids, expert_counts, tokens_total, capacity
    )
    slot_pairs = slot_index.reshape(tokens_total, 2)
    full_tokens = lax.all_gather(tokens, "tensor", axis=0, tiled=True)
    zero_row = jnp.zeros((1, full_tokens.shape[1]), full_tokens.dtype)
    rows = jnp.concatenate([full_tokens, zero_row], 0)[owner_token]
    gate_part = blocked_product(rows, w_gate, block_expert, False)
    up_part = blocked_product(rows, w_up, block_expert, False)
    gate, up = lax.psum((gate_part, up_part), "section")
    hidden = gate_forward(gate, up)
    out_rows = blocked_product(hidden, w_down, block_expert, False)
    token_terms = jnp.sum(combine[:, :, None] * out_rows[slot_pairs], 1)
    layer_out = lax.psum_scatter(token_terms, "tensor", scatter_dimension=0, tiled=True).astype(
        jnp.bfloat16
    )
    full_cot = lax.all_gather(cotangent, "tensor", axis=0, tiled=True)
    combine_slot = jnp.zeros((capacity,), jnp.float32).at[slot_index].set(combine.reshape(-1))
    cot_rows = jnp.concatenate([full_cot, zero_row], 0)[owner_token]
    row_grad = (combine_slot[:, None] * cot_rows.astype(jnp.float32)).astype(jnp.bfloat16)
    hidden_part = blocked_product(row_grad, w_down, block_expert, True)
    d_hidden = lax.psum(hidden_part, "section")
    d_gate, d_up = gate_backward(d_hidden, gate, up)
    nblocks = block_expert.shape[0]
    hidden_blocks = hidden.reshape(nblocks, BLOCK, hidden.shape[1])
    grad_blocks = row_grad.reshape(nblocks, BLOCK, row_grad.shape[1])
    block_terms = lax.dot_general(
        hidden_blocks, grad_blocks, (((1,), (1,)), ((0,), (0,))), preferred_element_type=jnp.float32
    )
    block_owner = (block_expert[None, :] == jnp.arange(EXPERTS, dtype=jnp.int32)[:, None]).astype(
        jnp.float32
    )
    d_down = jnp.einsum(
        "eb,bfd->efd", block_owner, block_terms, precision=lax.Precision.HIGHEST
    ).astype(jnp.bfloat16)
    d_rows = blocked_product(d_gate, w_gate, block_expert, True) + blocked_product(
        d_up, w_up, block_expert, True
    )
    grad_terms = jnp.sum(d_rows[slot_pairs], 1)
    d_tokens = lax.psum_scatter(grad_terms, "tensor", scatter_dimension=0, tiled=True).astype(
        jnp.bfloat16
    )
    return (layer_out, d_tokens, d_down)


def solution(mesh):
    in_specs = (
        P("tensor", "section"),
        P(),
        P(),
        P(),
        P(None, "section", "tensor"),
        P(None, "section", "tensor"),
        P(None, "tensor", "section"),
        P("tensor", "section"),
    )
    out_specs = (P("tensor", "section"), P("tensor", "section"), P(None, "tensor", "section"))
    return jax.shard_map(
        on_device, mesh=mesh, in_specs=in_specs, out_specs=out_specs, check_vma=False
    )
```

profile of v0, /device:TPU:1, one launch (start us, length us, event | category | flops | bytes accessed | tf_op | source)
XLA Modules:
  0.0 1162.6 jit_solution(10419398609167527737)
XLA Ops:
  8.3 27.5 %all_gather.6 = bf16[384,768]{1,0:T(8,128)(2,1)S(1)} all-gather(bf16[24,768]{1,0:T(8,128)(2,1)} %param.20), channel_id=1, replica_groups=mesh['section'=8,'tensor'=16] {'tensor'}, dimensions={0}, use_global_device_ids=true | all-gather | bytes 626688 | tf_op jit(solution)/shard_map/all_gather | solution.py:63
  39.1 3.4 scatter_custom_fusion
  42.7 4.2 gather_fusion
  46.9 3.0 broadcast.123.clone
  49.9 53.3 %while.61 = (s32[]{:T(128)}, f32[10,128,1024]{2,1,0:T(8,128)}, bf16[10,128,768]{2,1,0:T(8,128)(2,1)S(1)}, s32[10]{0:T(128)S(1)}, bf16[4,768,1024]{2,1,0:T(8,128)(2,1)}, /*index=5*/s32[]{:T(128)}, s32[]{:T(128)}, s32[]{:T(128)}) while((s32[]{:T(128)}, f32[10,128,1024]{2,1,0:T(8,128)}, bf16[10,128,768]{2,1,0:T(8,128)(2,1)S(1)}, ...), condition=%wide.region_11.12_spmd, body=%wide.region_10.11_spmd.sunk | while | flops 201326592 | bytes 2295435 | solution.py:40
  103.2 3.0 broadcast.123.clone.1
  106.2 51.4 %while.60 = (s32[]{:T(128)}, f32[10,128,1024]{2,1,0:T(8,128)}, bf16[10,128,768]{2,1,0:T(8,128)(2,1)S(1)}, s32[10]{0:T(128)S(1)}, bf16[4,768,1024]{2,1,0:T(8,128)(2,1)}, /*index=5*/s32[]{:T(128)}, s32[]{:T(128)}, s32[]{:T(128)}) while((s32[]{:T(128)}, f32[10,128,1024]{2,1,0:T(8,128)}, bf16[10,128,768]{2,1,0:T(8,128)(2,1)S(1)}, ...), condition=%wide.region_8.9_spmd, body=%wide.region_7.8_spmd.sunk | while | flops 201326592 | bytes 2295435 | solution.py:40
  157.7 20.9 %all_gather.7 = bf16[384,768]{1,0:T(8,128)(2,1)S(1)} all-gather(bf16[24,768]{1,0:T(8,128)(2,1)S(1)} %copy-done.1), channel_id=1, replica_groups=mesh['section'=8,'tensor'=16] {'tensor'}, dimensions={0}, use_global_device_ids=true | all-gather | bytes 626688 | tf_op jit(solution)/shard_map/all_gather | solution.py:75
  178.6 4.9 gather_fusion.2
  183.8 3.4 scatter_custom_fusion.1
  192.0 53.9 %while.63 = (s32[]{:T(128)}, f32[10,128,1024]{2,1,0:T(8,128)}, bf16[10,128,768]{2,1,0:T(8,128)(2,1)S(1)}, s32[10]{0:T(128)S(1)}, bf16[4,1024,768]{2,1,0:T(8,128)(2,1)}, /*index=5*/s32[]{:T(128)}, s32[]{:T(128)}, s32[]{:T(128)}) while((s32[]{:T(128)}, f32[10,128,1024]{2,1,0:T(8,128)}, bf16[10,128,768]{2,1,0:T(8,128)(2,1)S(1)}, ...), condition=%wide.region_19.20_spmd, body=%wide.region_18.19_spmd.sunk | while | flops 201326592 | bytes 2295435 | solution.py:40
  248.0 612.9 %all-reduce.5.cloned.1.call-done = (f32[1280,1024]{1,0:T(8,128)}, f32[1280,1024]{1,0:T(8,128)}, f32[1280,1024]{1,0:T(8,128)}) async-done(((f32[1280,1024]{1,0:T(8,128)}, f32[1280,1024]{1,0:T(8,128)}, f32[1280,1024]{1,0:T(8,128)}), (f32[1280,1024]{1,0:T(8,128)}, f32[1280,1024]{1,0:T(8,128)}, f32[1280,1024]{1,0:T(8,128)})) %all-reduce.5.cloned.1.call-update) | async-done | bytes 15728656 | tf_op jit(solution)/shard_map/psum | solution.py:68
  860.9 8.7 multiply_convert_fusion
  871.9 50.7 %while.62 = (s32[]{:T(128)}, f32[10,128,768]{2,1,0:T(8,128)}, bf16[10,128,1024]{2,1,0:T(8,128)(2,1)S(1)}, s32[10]{0:T(128)S(1)}, bf16[4,1024,768]{2,1,0:T(8,128)(2,1)}, /*index=5*/s32[]{:T(128)}, s32[]{:T(128)}, s32[]{:T(128)}) while((s32[]{:T(128)}, f32[10,128,768]{2,1,0:T(8,128)}, bf16[10,128,1024]{2,1,0:T(8,128)(2,1)S(1)}, ...), condition=%wide.region_14.15_spmd, body=%wide.region_13.14_spmd.sunk | while | flops 201326592 | bytes 2229899 | solution.py:40
  922.5 6.2 gather_fusion.1
  928.7 4.0 reshape.171
  932.7 5.6 multiply_reduce_fusion
  940.8 54.5 %while.64 = (s32[]{:T(128)}, f32[10,128,768]{2,1,0:T(8,128)}, bf16[10,128,1024]{2,1,0:T(8,128)(2,1)}, s32[10]{0:T(128)S(1)}, bf16[4,768,1024]{2,1,0:T(8,128)(2,1)}, /*index=5*/s32[]{:T(128)}, s32[]{:T(128)}, s32[]{:T(128)}) while((s32[]{:T(128)}, f32[10,128,768]{2,1,0:T(8,128)}, bf16[10,128,1024]{2,1,0:T(8,128)(2,1)}, s32[10]{0:T(128)S(1)}, ...), condition=%wide.region_22.23_spmd, body=%wide.region_21.22_spmd.sunk | while | flops 201326592 | bytes 2229899 | solution.py:40
  948.8 2.9 fusion.130
  954.3 2.9 fusion.130
  959.8 2.9 fusion.130
  997.6 54.4 %while.65 = (s32[]{:T(128)}, f32[10,128,768]{2,1,0:T(8,128)}, bf16[10,128,1024]{2,1,0:T(8,128)(2,1)}, s32[10]{0:T(128)S(1)}, bf16[4,768,1024]{2,1,0:T(8,128)(2,1)}, /*index=5*/s32[]{:T(128)}, s32[]{:T(128)}, s32[]{:T(128)}) while((s32[]{:T(128)}, f32[10,128,768]{2,1,0:T(8,128)}, bf16[10,128,1024]{2,1,0:T(8,128)(2,1)}, s32[10]{0:T(128)S(1)}, ...), condition=%wide.region_24.25_spmd, body=%wide.region_23.24_spmd.sunk | while | flops 201326592 | bytes 2229899 | solution.py:40
  1016.4 2.9 fusion.133
  1027.3 2.9 fusion.133
  1052.0 5.7 add.129
  1057.7 6.2 gather_fusion.3
  1063.9 4.0 reshape.191
  1067.9 5.5 reduce_sum.49
  1073.4 13.9 %fusion.94 = f32[10,1024,768]{2,1,0:T(8,128)} fusion(bf16[10,128,1024]{2,1,0:T(8,128)(2,1)S(1)} %get-tuple-element.589, bf16[10,128,768]{2,1,0:T(8,128)(2,1)} %copy-done), kind=kOutput, calls=%fused_computation.103 | convolution fusion | flops 2013265920 | bytes 36044800 | tf_op jit(solution)/shard_map/dot_general | solution.py:85
  1087.4 45.4 %fusion.74 = bf16[4,1024,768]{2,0,1:T(4,128)(2,1)S(1)} fusion(f32[10,1024,768]{2,1,0:T(8,128)} %fusion.94, s32[10]{0:T(128)S(1)} %get-tuple-element.611), kind=kOutput, calls=%fused_computation.60 | convolution fusion | flops 380633120 | bytes 37748776 | tf_op jit(solution)/shard_map/eb,bfd->efd/dot_general | solution.py:91
  1132.8 3.5 copy.24
  1137.8 16.5 %reduce-scatter.5.cloned.1.call-done = f32[24,768]{1,0:T(8,128)} async-done(((f32[384,768]{1,0:T(8,128)}), f32[24,768]{1,0:T(8,128)}) %reduce-scatter.5.cloned.1.call-update) | async-done | bytes 73744 | tf_op jit(solution)/shard_map/reduce_scatter | solution.py:98
  (163 shorter events, 207.9 us)
Async XLA Ops:
  7.2 853.7 %all-reduce.5.cloned.1.call-start = ((), (), s32[]{:S(2)}) async-start(), calls=%async_computation.4 | async-start | bytes 31457280 | tf_op jit(solution)/shard_map/psum | solution.py:68
  106.2 51.4 %copy-start.1 = (bf16[24,768]{1,0:T(8,128)(2,1)S(1)}, bf16[24,768]{1,0:T(8,128)(2,1)}, u32[]{:S(2)}) copy-start(bf16[24,768]{1,0:T(8,128)(2,1)} %param.27) | copy-start | bytes 110596
  178.6 4.9 copy-start.2
  245.9 1.3 copy-start
  247.1 889.2 %reduce-scatter.3.cloned.1.call-start = ((), (), s32[]{:S(2)}) async-start(), calls=%async_computation.2 | async-start | bytes 1253376 | tf_op jit(solution)/shard_map/reduce_scatter | solution.py:72
  938.3 216.0 %reduce-scatter.5.cloned.1.call-start = ((), (), s32[]{:S(2)}) async-start(), calls=%async_computation.3 | async-start | bytes 1253376 | tf_op jit(solution)/shard_map/reduce_scatter | solution.py:98
Sparse Core Ops, SparseCore 0:
  246.0 614.8 all-reduce.4
  938.5 66.7 reduce-scatter.2
  1087.5 66.7 reduce-scatter.4
where the time goes:
time: 1170 us; the launch traced here: 1160 us
  waiting for transfers between devices  629 us (54%)
  matrix products  224 us (19%)
  loops' own time  117 us (10%)
  local copies, waits for them, and re-layouts  94.9 us (8%)
  blocking collectives  48.4 us (4%)
  other arithmetic  33.6 us (3%)
  between operations  14.1 us (1%)
    psum x1, waiting for transfers between devices, on_device(): gate, up = lax.psum((gate_part, up_part), 'section')  613 us
    another operation x6, loops' own time, blocked_product(): result = lax.map(apply_block, (blocks, block_expert))  117 us
    dot_general x30, matrix products, apply_block(): lax.dot_general(segment, matrix, (((1,), (1,)), ((), ())), preferred_elem...  87 us
    dot_general x30, matrix products, apply_block(): return jnp.dot(segment, matrix, preferred_element_type=jnp.float32)  77.5 us
    dot_general x1, matrix products, on_device(): jnp.einsum('eb,bfd->efd', block_owner, block_terms, precision=lax.Precisi...  45.4 us
    dynamic_slice x60, local copies, waits for them, and re-layouts, blocked_product(): result = lax.map(apply_block, (blocks, block_expert))  36.3 us
    all_gather x1, blocking collectives, on_device(): full_tokens = lax.all_gather(tokens, 'tensor', axis=0, tiled=True)  27.5 us
  transfers between devices with their start and end apart: 3, of which 2 were waited for; matrix products, arithmetic and copies ran while one was open for 14% of the time, Pallas kernels for 0%

commit v1 on v0

v1 whole, which is shorter than its diff:
```python
import jax
import jax.numpy as jnp
from jax import lax
from jax.sharding import PartitionSpec as P

EXPERTS = 4


def on_device(tokens, combine, expert_ids, expert_counts, w_gate, w_up, w_down, cotangent):
    total = combine.shape[0]
    both = lax.all_gather(jnp.stack([tokens, cotangent]), "tensor", axis=1, tiled=True)
    x, cot = both[0], both[1].astype(jnp.float32)
    common = jnp.argmax(expert_counts == total).astype(jnp.int32)
    is_common = expert_ids == common
    comb_c = jnp.sum(jnp.where(is_common, combine, 0.0), 1)[:, None]
    comb_o = jnp.sum(jnp.where(is_common, 0.0, combine), 1)[:, None]
    other = jnp.sum(jnp.where(is_common, 0, expert_ids), 1)
    mask_o = [(other == e)[:, None] for e in range(EXPERTS)]
    rg_c = (comb_c * cot).astype(jnp.bfloat16)
    rg_o = (comb_o * cot).astype(jnp.bfloat16)

    def pick(rows):
        return jnp.concatenate([jnp.where(m, rows, jnp.zeros_like(rows)) for m in mask_o], 1)

    def dot(a, b, dims):
        return lax.dot_general(a, b, (dims, ((), ())), preferred_element_type=jnp.float32)

    d_loc, f_loc = w_gate.shape[1:]
    x_o = pick(x).reshape(total, EXPERTS, d_loc)
    g_o = pick(rg_o).reshape(total, EXPERTS, d_loc)
    take = lambda w: lax.dynamic_index_in_dim(w, common, 0, keepdims=False)
    gate_c = dot(x, take(w_gate), ((1,), (0,)))
    up_c = dot(x, take(w_up), ((1,), (0,)))
    dh_c = dot(rg_c, take(w_down), ((1,), (1,)))
    gate_o = dot(x_o, w_gate, ((1, 2), (0, 1)))
    up_o = dot(x_o, w_up, ((1, 2), (0, 1)))
    dh_o = dot(g_o, w_down, ((1, 2), (0, 2)))
    parts = jnp.stack([gate_c, gate_o, up_c, up_o, dh_c, dh_o]).astype(jnp.bfloat16)
    nsec = lax.axis_size("section")
    parts = parts.reshape(6, total, nsec, f_loc // nsec).transpose(2, 0, 1, 3)
    sums = lax.all_to_all(parts, "section", 0, 0, tiled=True).astype(jnp.float32).sum(0)
    gate, up, dh = sums[0:2], sums[2:4], sums[4:6]
    s = jax.nn.sigmoid(gate)
    act = gate * s
    mine = jnp.stack([act * up, dh * up * s * (1.0 + gate * (1.0 - s)), dh * act]).astype(jnp.bfloat16)
    full = lax.all_gather(mine, "section", axis=0)
    full = full.transpose(1, 2, 3, 0, 4).reshape(3, 2, total, f_loc)
    (h_c, h_o), (dg_c, dg_o), (du_c, du_o) = full[0], full[1], full[2]

    def pick_all(rows_c, rows_o):
        return [
            jnp.where(common == e, rows_c, jnp.where(mask_o[e], rows_o, jnp.zeros_like(rows_o)))
            for e in range(EXPERTS)
        ]

    hs, dgs, dus = pick_all(h_c, h_o), pick_all(dg_c, dg_o), pick_all(du_c, du_o)
    out = jnp.zeros((total, d_loc), jnp.float32)
    dtok = jnp.zeros((total, d_loc), jnp.float32)
    d_down = []
    for e in range(EXPERTS):
        comb_e = jnp.where(common == e, comb_c, comb_o)
        out += comb_e * dot(hs[e], w_down[e], ((1,), (0,)))
        dtok += dot(dgs[e], w_gate[e], ((1,), (1,))) + dot(dus[e], w_up[e], ((1,), (1,)))
        rg_e = jnp.where(common == e, rg_c, rg_o)
        d_down.append(dot(hs[e], rg_e, ((0,), (0,))).astype(jnp.bfloat16))
    res = lax.psum_scatter(jnp.stack([out, dtok]), "tensor", scatter_dimension=1, tiled=True)
    res = res.astype(jnp.bfloat16)
    return res[0], res[1], jnp.stack(d_down)


def solution(mesh):
    in_specs = (
        P("tensor", "section"),
        P(),
        P(),
        P(),
        P(None, "section", "tensor"),
        P(None, "section", "tensor"),
        P(None, "tensor", "section"),
        P("tensor", "section"),
    )
    out_specs = (P("tensor", "section"), P("tensor", "section"), P(None, "tensor", "section"))
    return jax.shard_map(
        on_device, mesh=mesh, in_specs=in_specs, out_specs=out_specs, check_vma=False
    )
```

time: 1170 us -> 353 us (0.30)
  waiting for transfers between devices: 629 us -> 195 us
  matrix products: 224 us -> 33.6 us
  loops' own time: 117 us -> 0 us
  local copies, waits for them, and re-layouts: 94.9 us -> 26.5 us
  other arithmetic: 33.6 us -> 18.6 us
    psum x1 -> x0, waiting for transfers between devices: 613 us -> none  [on_device(): gate, up = lax.psum((gate_part, up_part), 'section')]
    dot_general x62 -> x22, matrix products: 224 us -> 33.6 us  [dot(): lax.dot_general(a, b, (dims, ((), ())), preferred_element_type=jnp.float32)]
    all_gather x0 -> x2, waiting for transfers between devices: none -> 134 us  [the longest x1 95.8 us: on_device(): full = lax.all_gather(mine, 'section', axis=0)]
    another operation x6 -> x0, loops' own time: 117 us -> none  [blocked_product(): result = lax.map(apply_block, (blocks, block_expert))]
    all_to_all x0 -> x1, blocking collectives: none -> 58.2 us  [on_device(): lax.all_to_all(parts, 'section', 0, 0, tiled=True).astype(jnp.float32)]
    all_gather x2 -> x0, blocking collectives: 48.4 us -> none  [the longest x1 27.5 us: on_device(): full_tokens = lax.all_gather(tokens, 'tensor', axis=0, tiled=True)]
    reduce_scatter x2 -> x1, waiting for transfers between devices: 16.5 us -> 61.6 us  [on_device(): lax.psum_scatter(jnp.stack([out, dtok]), 'tensor', scatter_dimension=1, t...]
    dynamic_slice x60 -> x1, local copies, waits for them, and re-layouts: 36.3 us -> 2.66 us  [on_device(): take = lambda w: lax.dynamic_index_in_dim(w, common, 0, keepdims=False)]
  transfers between devices with their start and end apart: 3 -> 3, of which waited for: 2 -> 3; matrix products, arithmetic and copies ran while one was open for 14% -> 6% of each run, Pallas kernels for 0% -> 0%
where the time goes in v1:
time: 353 us; the launch traced here: 351 us
  waiting for transfers between devices  195 us (55%)
  blocking collectives  58.2 us (16%)
  matrix products  33.6 us (10%)
  local copies, waits for them, and re-layouts  26.5 us (8%)
  between operations  18.8 us (5%)
  other arithmetic  18.6 us (5%)
    all_gather x1, waiting for transfers between devices, on_device(): full = lax.all_gather(mine, 'section', axis=0)  95.8 us
    reduce_scatter x1, waiting for transfers between devices, on_device(): lax.psum_scatter(jnp.stack([out, dtok]), 'tensor', scatter_dimension=1, t...  61.6 us
    all_to_all x1, blocking collectives, on_device(): lax.all_to_all(parts, 'section', 0, 0, tiled=True).astype(jnp.float32)  58.2 us
    all_gather x1, waiting for transfers between devices, on_device(): lax.all_gather(jnp.stack([tokens, cotangent]), 'tensor', axis=1, tiled=True)  37.8 us
    dot_general x22, matrix products, dot(): lax.dot_general(a, b, (dims, ((), ())), preferred_element_type=jnp.float32)  33.6 us
    unnamed x64, local copies, waits for them, and re-layouts  8.36 us
  transfers between devices with their start and end apart: 3, of which 3 were waited for; matrix products, arithmetic and copies ran while one was open for 6% of the time, Pallas kernels for 0%

profile of v1, /device:TPU:1, one launch (start us, length us, event | category | flops | bytes accessed | tf_op | source)
XLA Modules:
  0.0 351.0 jit_solution(4337328475377516094)
XLA Ops:
  7.2 1.4 pad_maximum_fusion.6
  8.7 1.3 compare_reduce_fusion
  12.0 2.2 dynamic-slice_bitcast_fusion
  14.1 1.6 copy.41
  15.7 1.6 copy.43
  18.7 2.7 constant_dynamic-slice_fusion
  21.4 37.8 %all-gather.3.cloned.1.call-done = bf16[2,384,768]{2,1,0:T(8,128)(2,1)} async-done(((bf16[2,24,768]{2,1,0:T(8,128)(2,1)}), bf16[2,384,768]{2,1,0:T(8,128)(2,1)}) %all-gather.3.cloned.1.call-update) | async-done | bytes 1179664 | tf_op jit(solution)/shard_map/all_gather | solution.py:11
  59.2 2.9 broadcast_select_fusion.3
  62.0 5.6 %bitcast_convert_fusion.2 = bf16[384,1024]{1,0:T(8,128)(2,1)S(1)} fusion(bf16[4,768,1024]{2,1,0:T(8,128)(2,1)} %param.12, bf16[384,1,768]{2,0,1:T(8,128)(2,1)S(1)} %get-tuple-element.29, bf16[384,1,768]{2,0,1:T(8,128)(2,1)S(1)} %get-tuple-element.30, bf16[384,1,768]{2,0,1:T(8,128)(2,1)S(1)} %get-tuple-element.31, bf16[384,1,768]{2,0,1:T(8,128)(2,1)S(1)} %get-tuple-element.32), kind=kOutput, calls=%fused_computation.45 | convolution fusion | flops 2419851264 | bytes 9437184 | tf_op jit(solution)/shard_map/dot_general | solution.py:26
  67.6 2.6 bitcast_convert_fusion.1
  72.6 5.8 %bitcast_convert_fusion = bf16[384,1024]{1,0:T(8,128)(2,1)S(1)} fusion(bf16[4,1024,768]{2,1,0:T(8,128)(2,1)} %param.14, bf16[384,1,768]{2,0,1:T(8,128)(2,1)} %get-tuple-element.28, bf16[384,1,768]{2,0,1:T(8,128)(2,1)} %get-tuple-element.27, bf16[384,1,768]{2,0,1:T(8,128)(2,1)S(1)} %copy-done.11, bf16[384,1,768]{2,0,1:T(8,128)(2,1)S(1)} %copy-done.10), kind=kOutput, calls=%fused_computation.43 | convolution fusion | flops 2419851264 | bytes 9437184 | tf_op jit(solution)/shard_map/dot_general | solution.py:26
  79.2 2.5 fusion.99
  81.8 1.3 copy-done.1
  83.1 1.0 fusion.101
  84.3 1.3 copy-done.2
  85.6 1.0 fusion.103
  87.3 58.2 %all_to_all.5 = bf16[8,6,384,128]{3,2,1,0:T(8,128)(2,1)S(1)} all-to-all(bf16[8,6,384,128]{3,2,1,0:T(8,128)(2,1)S(1)} %copy.49), channel_id=1, replica_groups=mesh['section'=8,'tensor'=16] {'section'}, dimensions={0} | all-to-all | bytes 9437184 | tf_op jit(solution)/shard_map/all_to_all | solution.py:41
  150.5 95.8 %all-gather.5.cloned.1.call-done = bf16[8,3,2,384,128]{4,3,2,1,0:T(8,128)(2,1)} async-done(((bf16[1,3,2,384,128]{4,3,2,1,0:T(8,128)(2,1)}), bf16[8,3,2,384,128]{4,3,2,1,0:T(8,128)(2,1)}) %all-gather.5.cloned.1.call-update) | async-done | bytes 4718608 | tf_op jit(solution)/shard_map/all_gather | solution.py:46
  246.3 6.6 %copy.50 = bf16[8,3,2,384,128]{3,4,0,2,1:T(8,128)(2,1)} copy(bf16[8,3,2,384,128]{4,3,2,1,0:T(8,128)(2,1)} %all-gather.5.cloned.1.call-done) | data formatting | bytes 9437184 | tf_op jit(solution)/shard_map/all_gather | solution.py:46
  253.0 3.1 select_select_fusion.11
  257.3 1.0 slice-done.6
  258.3 1.3 slice-done.7
  267.9 0.9 fusion.77
  270.5 1.6 pad_maximum_fusion.2
  272.1 1.1 copy-done.9
  273.2 1.2 fusion.47
  274.4 1.4 fusion.46
  275.9 1.2 fusion.45
  277.0 1.2 fusion.44
  278.2 3.2 pad_maximum_fusion
  281.4 61.6 %reduce-scatter.2.cloned.1.call-done = f32[2,24,768]{2,1,0:T(8,128)} async-done(((f32[2,384,768]{2,1,0:T(8,128)}), f32[2,24,768]{2,1,0:T(8,128)}) %reduce-scatter.2.cloned.1.call-update) | async-done | bytes 147472 | tf_op jit(solution)/shard_map/reduce_scatter | solution.py:66
  343.0 0.9 convert_element_type.102
  (97 shorter events, 19.6 us)
Async XLA Ops:
  7.2 52.0 %all-gather.3.cloned.1.call-start = ((), (), s32[]{:S(2)}) async-start(), calls=%async_computation.2 | async-start | bytes 1253376 | tf_op jit(solution)/shard_map/all_gather | solution.py:11
  8.7 237.7 %all-gather.5.cloned.1.call-start = ((), (), s32[]{:S(2)}) async-start(), calls=%async_computation.3 | async-start | bytes 5308416 | tf_op jit(solution)/shard_map/all_gather | solution.py:46
  15.7 1.6 copy-start.12
  15.7 2.3 copy-start.19
  21.4 40.7 %copy-start.13 = (pred[384]{0:T(512)(128)(4,1)}, pred[384]{0:T(512)(128)(4,1)S(1)}, u32[]{:S(2)}) copy-start(pred[384]{0:T(512)(128)(4,1)S(1)} %get-tuple-element.45) | copy-start | bytes 1156
  21.4 40.7 %copy-start.15 = (pred[384]{0:T(512)(128)(4,1)}, pred[384]{0:T(512)(128)(4,1)S(1)}, u32[]{:S(2)}) copy-start(pred[384]{0:T(512)(128)(4,1)S(1)} %get-tuple-element.42) | copy-start | bytes 1156
  21.4 40.7 %copy-start.17 = (pred[384]{0:T(512)(128)(4,1)}, pred[384]{0:T(512)(128)(4,1)S(1)}, u32[]{:S(2)}) copy-start(pred[384]{0:T(512)(128)(4,1)S(1)} %get-tuple-element.44) | copy-start | bytes 1156
  59.2 8.5 %slice-start.4 = ((s8[6291456]{0:T(1024)(128)(4,1)}), s8[4194304]{0:T(1024)(128)(4,1)S(1)}, s32[]{:S(2)}) async-start(s8[6291456]{0:T(1024)(128)(4,1)} %bitcast.230), calls=%async_computation.9 | async-start | bytes 8388608
  62.0 5.6 %slice-start.5 = ((s8[6291456]{0:T(1024)(128)(4,1)}), s8[2097152]{0:T(1024)(128)(4,1)S(1)}, s32[]{:S(2)}) async-start(s8[6291456]{0:T(1024)(128)(4,1)} %bitcast.230), calls=%async_computation.10 | async-start | bytes 4194304
  71.4 1.1 copy-start.10
  71.4 1.2 copy-start.11
  79.2 2.6 copy-start.3
  81.7 1.4 copy-start.1
  84.2 1.4 copy-start.2
  147.3 195.7 %reduce-scatter.2.cloned.1.call-start = ((), (), s32[]{:S(2)}) async-start(), calls=%async_computation.4 | async-start | bytes 2506752 | tf_op jit(solution)/shard_map/reduce_scatter | solution.py:66
  150.5 102.4 %copy-start.16 = (pred[384]{0:T(512)(128)(4,1)S(1)}, pred[384]{0:T(512)(128)(4,1)}, u32[]{:S(2)}) copy-start(pred[384]{0:T(512)(128)(4,1)} %copy-done.15) | copy-start | bytes 1156
  150.5 102.4 %copy-start.18 = (pred[384]{0:T(512)(128)(4,1)S(1)}, pred[384]{0:T(512)(128)(4,1)}, u32[]{:S(2)}) copy-start(pred[384]{0:T(512)(128)(4,1)} %copy-done.17) | copy-start | bytes 1156
  252.9 3.8 %copy-start = (bf16[8,3,2,384,128]{3,4,0,2,1:T(8,128)(2,1)S(1)}, bf16[8,3,2,384,128]{3,4,0,2,1:T(8,128)(2,1)}, u32[]{:S(2)}) copy-start(bf16[8,3,2,384,128]{3,4,0,2,1:T(8,128)(2,1)} %copy.50) | copy-start | bytes 14155780
  252.9 3.8 %copy-start.14 = (pred[384]{0:T(512)(128)(4,1)S(1)}, pred[384]{0:T(512)(128)(4,1)}, u32[]{:S(2)}) copy-start(pred[384]{0:T(512)(128)(4,1)} %copy-done.13) | copy-start | bytes 1156
  253.0 5.3 %slice-start.6 = ((s8[6291456]{0:T(1024)(128)(4,1)}), s8[4194304]{0:T(1024)(128)(4,1)S(1)}, s32[]{:S(2)}) async-start(s8[6291456]{0:T(1024)(128)(4,1)} %bitcast.232), calls=%async_computation.11 | async-start | bytes 8388608
  256.7 9.5 %copy-start.4 = (bf16[1,1,384,8,128]{2,4,3,1,0:T(8,128)(2,1)}, bf16[1,1,384,8,128]{2,4,3,1,0:T(8,128)(2,1)S(1)}, u32[]{:S(2)}) copy-start(bf16[1,1,384,8,128]{2,4,3,1,0:T(8,128)(2,1)S(1)} %get-tuple-element.21) | copy-start | bytes 2359300
  256.7 2.9 slice-start.7
  257.3 8.0 %copy-start.8 = (bf16[1,1,384,8,128]{2,4,3,1,0:T(8,128)(2,1)}, bf16[1,1,384,8,128]{2,4,3,1,0:T(8,128)(2,1)S(1)}, u32[]{:S(2)}) copy-start(bf16[1,1,384,8,128]{2,4,3,1,0:T(8,128)(2,1)S(1)} %get-tuple-element.24) | copy-start | bytes 2359300
  257.3 9.7 %copy-start.6 = (bf16[1,1,384,8,128]{2,4,3,1,0:T(8,128)(2,1)}, bf16[1,1,384,8,128]{2,4,3,1,0:T(8,128)(2,1)S(1)}, u32[]{:S(2)}) copy-start(bf16[1,1,384,8,128]{2,4,3,1,0:T(8,128)(2,1)S(1)} %get-tuple-element.10) | copy-start | bytes 2359300
  260.4 2.6 slice-start
  261.3 2.2 slice-start.1
  262.1 3.1 slice-start.2
  263.5 1.8 slice-start.3
  264.4 1.0 copy-start.22
  272.1 1.1 copy-start.9
  273.2 1.2 copy-start.5
  274.4 1.4 copy-start.7
  (2 other events, 1.7 us)
Sparse Core Ops, SparseCore 0:
  10.4 48.7 all-gather.2
  147.4 98.8 all-gather.4
  272.2 70.6 reduce-scatter.1

commit v2 on v1

v2 whole, which is shorter than its diff:
```python
import jax
import jax.numpy as jnp
from jax import lax
from jax.experimental import pallas as pl
from jax.experimental.pallas import tpu as pltpu
from jax.sharding import PartitionSpec as P

EXPERTS = 4
NZ = 4
BF = jnp.bfloat16
F32 = jnp.float32
MESH = pl.DeviceIdType.MESH


def mm(a, b):
    return jnp.dot(a, b, preferred_element_type=F32)


def mm_nt(a, b):
    return lax.dot_general(a, b, (((1,), (1,)), ((), ())), preferred_element_type=F32)


def mm_tn(a, b):
    return lax.dot_general(a, b, (((0,), (0,)), ((), ())), preferred_element_type=F32)


def layer_kernel(
    c_ref, meta_ref, xt_ref, wg_hbm, wu_hbm, wd_hbm,
    lo_ref, dt_ref, dd_hbm,
    wgu, wd, xbuf, xf, cf, xs, xm, rgc, rgo, rgm, mo, cb,
    pa, paf, pb, pbf, rar, raf, sa, ray, rby, qb, rbr, rbf, hc, ho, dd, fs, fr, gs, gr,
    w_sem, loc_sem, x_send, x_recv, a_send, a_recv, b_send, b_recv,
    c_send, c_recv, o_send, o_recv, dd_sem, f_send, f_recv,
):
    tokens, dloc = xf.shape
    fc = pa.shape[-1]
    half = tokens // 2
    quart = half // 2
    bl = tokens // 16
    nt = dloc // 256

    s = lax.axis_index("section")
    t = lax.axis_index("tensor")
    z, yl = s // 2, s % 2
    zp = ((z + 1) % NZ) * 2 + yl
    zm = ((z + 3) % NZ) * 2 + yl
    yp = z * 2 + 1 - yl
    core, kt, x = t % 2, t // 2, t // 4
    yh = kt % 2

    def tx(d):
        return ((x + d) % 4) * 4 + yh * 2 + core

    ty = x * 4 + (1 - yh) * 2 + core
    sib = t + 1 - 2 * core

    def sec(src, dst, ssem, rsem, dev):
        return pltpu.make_async_remote_copy(src, dst, ssem, rsem, {"section": dev}, MESH)

    def ten(src, dst, ssem, rsem, dev):
        return pltpu.make_async_remote_copy(src, dst, ssem, rsem, {"tensor": dev}, MESH)

    for e in range(EXPERTS):
        pltpu.make_async_copy(wg_hbm.at[e], wgu.at[0, e], w_sem.at[0, e]).start()
        pltpu.make_async_copy(wu_hbm.at[e], wgu.at[1, e], w_sem.at[1, e]).start()
        pltpu.make_async_copy(wd_hbm.at[e], wd.at[e], w_sem.at[2, e]).start()

    barrier = pltpu.get_barrier_semaphore()
    for dev in (zp, zm, yp):
        pl.semaphore_signal(barrier, inc=1, device_id={"section": dev}, device_id_type=MESH)
    for k in range(1, 8):
        pl.semaphore_signal(
            barrier, inc=1, device_id={"tensor": ((kt + k) % 8) * 2 + core}, device_id_type=MESH
        )
    pl.semaphore_signal(barrier, inc=1, device_id={"tensor": sib}, device_id_type=MESH)
    pl.semaphore_wait(barrier, 11)

    q = core * 8 + kt
    qy = core * 8 + x * 2 + 1 - yh
    own_copy = pltpu.make_async_copy(xt_ref, xbuf.at[q], loc_sem)
    own_copy.start()
    targets = (ty, tx(1), tx(3), tx(2), sib)
    own_sends = [
        ten(xt_ref, xbuf.at[q], x_send.at[i], x_recv.at[q], dev) for i, dev in enumerate(targets)
    ]
    for cp in own_sends:
        cp.start()

    def x_wait(slot):
        ten(xt_ref, xbuf.at[slot], x_send.at[0], x_recv.at[slot], sib).wait_recv()

    x_wait(qy)
    fwd_sends = [
        ten(xbuf.at[qy], xbuf.at[qy], x_send.at[5 + i], x_recv.at[qy], dev)
        for i, dev in enumerate(targets[1:])
    ]
    for cp in fwd_sends:
        cp.start()
    n = 9
    for flip in (0, 1):
        for d in (1, 3, 2):
            other_y = yh + flip - 2 * yh * flip
            slot = core * 8 + ((x + d) % 4) * 2 + other_y
            x_wait(slot)
            cp = ten(xbuf.at[slot], xbuf.at[slot], x_send.at[n], x_recv.at[slot], sib)
            cp.start()
            fwd_sends.append(cp)
            n += 1
    for k in range(8):
        x_wait((1 - core) * 8 + k)
    own_copy.wait()

    def split(i, carry):
        rows = pl.ds(pl.multiple_of(i * bl, 8), bl)
        v = xbuf[i].astype(F32)
        xf[rows, :] = v[:bl]
        cf[rows, :] = v[bl:]
        return carry

    lax.fori_loop(0, 16, split, 0)

    common = c_ref[0]
    others = [(common + 1 + j) % EXPERTS for j in range(EXPERTS - 1)]
    rt = 32

    def prep(i, carry):
        rows = pl.ds(pl.multiple_of(i * rt, rt), rt)
        m = meta_ref[rows, :]
        cc, co, oid = m[:, 0:1], m[:, 1:2], m[:, 2:3]
        xv, cv = xf[rows, :], cf[rows, :]
        rc = (cc * cv).astype(BF).astype(F32)
        ro = (co * cv).astype(BF).astype(F32)
        xs[rows, :] = xv.astype(BF)
        rgc[rows, :] = rc.astype(BF)
        rgo[rows, :] = ro.astype(BF)
        for j, e in enumerate(others):
            hit = oid == e.astype(F32)
            xm[j, rows, :] = jnp.where(hit, xv, 0.0).astype(BF)
            rgm[j, rows, :] = jnp.where(hit, ro, 0.0).astype(BF)
        for e in range(EXPERTS):
            hit = (oid == float(e)).astype(F32)
            mo[e, rows, :] = jnp.broadcast_to(hit, (rt, fc)).astype(BF)
        cb[0, rows, :] = jnp.broadcast_to(cc, (rt, 256))
        cb[1, rows, :] = jnp.broadcast_to(co, (rt, 256))
        return carry

    lax.fori_loop(0, tokens // rt, prep, 0)

    for e in range(EXPERTS):
        pltpu.make_async_copy(wg_hbm.at[e], wgu.at[0, e], w_sem.at[0, e]).wait()
        pltpu.make_async_copy(wu_hbm.at[e], wgu.at[1, e], w_sem.at[1, e]).wait()
        pltpu.make_async_copy(wd_hbm.at[e], wd.at[e], w_sem.at[2, e]).wait()

    my = pl.ds(pl.multiple_of(yl * half, half), half)
    his = pl.ds(pl.multiple_of((1 - yl) * half, half), half)
    h1, h2 = pl.ds(0, half), pl.ds(half, half)
    q1, q2 = pl.ds(0, quart), pl.ds(quart, quart)

    def by(r):
        return sec(pb.at[r, :, his], rby.at[r], b_send.at[r], b_recv.at[r], yp)

    ar0 = sec(pa.at[0, :, h1], rar.at[0], a_send.at[0], a_recv.at[0], zp)
    ar1 = sec(pa.at[0, :, h2], rar.at[1], a_send.at[1], a_recv.at[1], zm)
    af0b = sec(pa.at[1, :, h2], raf.at[0, :, h2], a_send.at[2], a_recv.at[2], zp)
    af0a = sec(pa.at[1, :, h1], raf.at[0, :, h1], a_send.at[3], a_recv.at[3], zp)
    af1a = sec(pa.at[2, :, h1], raf.at[1, :, h1], a_send.at[4], a_recv.at[4], zm)
    af1b = sec(pa.at[2, :, h2], raf.at[1, :, h2], a_send.at[5], a_recv.at[5], zm)
    ay = sec(sa, ray, a_send.at[6], a_recv.at[6], yp)

    def chunk(r, carry):
        off = 2 - r + 3 * (r // 2) - 2 * (r // 3)
        zc = (z + off) % NZ
        cols = pl.ds(pl.multiple_of(zc * fc, fc), fc)

        def proj_o(a, c2):
            acc = mm(xm[0], wgu[a, others[0], :, cols])
            acc += mm(xm[1], wgu[a, others[1], :, cols])
            acc += mm(xm[2], wgu[a, others[2], :, cols])
            pbf[r, a] = acc
            pb[r, a] = acc.astype(BF)
            return c2

        lax.fori_loop(0, 2, proj_o, 0)
        acc = mm_nt(rgm[0], wd[others[0], cols, :])
        acc += mm_nt(rgm[1], wd[others[1], cols, :])
        acc += mm_nt(rgm[2], wd[others[2], cols, :])
        pbf[r, 2] = acc
        pb[r, 2] = acc.astype(BF)
        by(r).start()

        def proj_c(a, c2):
            acc = mm(xs[...], wgu[a, common, :, cols])
            paf[r, a] = acc
            pa[r, a] = acc.astype(BF)
            return c2

        lax.fori_loop(0, 2, proj_c, 0)
        acc = mm_nt(rgc[...], wd[common, cols, :])
        paf[r, 2] = acc
        pa[r, 2] = acc.astype(BF)

        @pl.when(r == 0)
        def _():
            ar0.start()
            ar1.start()

        @pl.when(r == 1)
        def _():
            af0b.start()

        @pl.when(r == 2)
        def _():
            af1a.start()

        return carry

    lax.fori_loop(0, NZ, chunk, 0)

    ar0.wait_recv()
    pa[1, :, h1] = (paf[1, :, h1] + rar[0].astype(F32)).astype(BF)
    af0a.start()
    ar1.wait_recv()
    pa[2, :, h2] = (paf[2, :, h2] + rar[1].astype(F32)).astype(BF)
    af1b.start()

    br0 = sec(qb.at[0, :, q1], rbr.at[0], b_send.at[4], b_recv.at[4], zp)
    br1 = sec(qb.at[0, :, q2], rbr.at[1], b_send.at[5], b_recv.at[5], zm)
    bf0b = sec(qb.at[1, :, q2], rbf.at[0, :, q2], b_send.at[6], b_recv.at[6], zp)
    bf0a = sec(qb.at[1, :, q1], rbf.at[0, :, q1], b_send.at[7], b_recv.at[7], zp)
    bf1a = sec(qb.at[2, :, q1], rbf.at[1, :, q1], b_send.at[8], b_recv.at[8], zm)
    bf1b = sec(qb.at[2, :, q2], rbf.at[1, :, q2], b_send.at[9], b_recv.at[9], zm)
    myq1 = pl.ds(pl.multiple_of(yl * half, quart), quart)
    myq2 = pl.ds(pl.multiple_of(yl * half + quart, quart), quart)

    by(0).wait_recv()
    qb[0] = (pbf[0, :, my] + rby[0].astype(F32)).astype(BF)
    br0.start()
    br1.start()
    by(1).wait_recv()
    qb[1, :, q2] = (pbf[1, :, myq2] + rby[1, :, q2].astype(F32)).astype(BF)
    bf0b.start()
    br0.wait_recv()
    qb[1, :, q1] = (
        pbf[1, :, myq1] + rby[1, :, q1].astype(F32) + rbr[0].astype(F32)
    ).astype(BF)
    bf0a.start()
    by(2).wait_recv()
    qb[2, :, q1] = (pbf[2, :, myq1] + rby[2, :, q1].astype(F32)).astype(BF)
    bf1a.start()
    br1.wait_recv()
    qb[2, :, q2] = (
        pbf[2, :, myq2] + rby[2, :, q2].astype(F32) + rbr[1].astype(F32)
    ).astype(BF)
    bf1b.start()
    for cp in (af0b, af0a, af1a, af1b):
        cp.wait_recv()
    sa[...] = (
        paf[3, :, his] + raf[0, :, his].astype(F32) + raf[1, :, his].astype(F32)
    ).astype(BF)
    ay.start()

    def swiglu(total, dst):
        gate, up, dh = total(0), total(1), total(2)
        sg = 1.0 / (1.0 + jnp.exp(-gate))
        act = gate * sg
        dst[z, 0, my, :] = (act * up).astype(BF)
        dst[z, 1, my, :] = (dh * up * sg * (1.0 + gate * (1.0 - sg))).astype(BF)
        dst[z, 2, my, :] = (dh * act).astype(BF)

    by(3).wait_recv()
    for cp in (bf0b, bf0a, bf1a, bf1b):
        cp.wait_recv()
    swiglu(
        lambda a: pbf[3, a, my, :]
        + rby[3, a].astype(F32)
        + rbf[0, a].astype(F32)
        + rbf[1, a].astype(F32),
        ho,
    )

    z1, z3, z2 = (z + 1) % NZ, (z + 3) % NZ, (z + 2) % NZ

    def oz(zc, d, dev):
        return sec(ho.at[zc, :, my], ho.at[zc, :, my], o_send.at[d], o_recv.at[d], dev)

    def oy(zc, i, rows):
        return sec(ho.at[zc, :, rows], ho.at[zc, :, rows], o_send.at[4 + i], o_recv.at[4 + i], yp)

    def orl(zc, rows, d, dev):
        return sec(ho.at[zc, :, rows], ho.at[zc, :, rows], o_send.at[2 + d], o_recv.at[2 + d], dev)

    oz(z, 0, zp).start()
    oz(z, 1, zm).start()
    oy(z, 0, my).start()

    ay.wait_recv()
    swiglu(
        lambda a: paf[3, a, my, :]
        + raf[0, a, my, :].astype(F32)
        + raf[1, a, my, :].astype(F32)
        + ray[a].astype(F32),
        hc,
    )

    def cy(rows):
        return sec(hc.at[z, :, rows], hc.at[z, :, rows], c_send.at[0], c_recv.at[0], yp)

    def cz(zc, h, rows, d, dev):
        i = 1 + 2 * d + h
        return sec(hc.at[zc, :, rows], hc.at[zc, :, rows], c_send.at[i], c_recv.at[i], dev)

    def crl(zc, rows, d, dev):
        return sec(hc.at[zc, :, rows], hc.at[zc, :, rows], c_send.at[5 + d], c_recv.at[5 + d], dev)

    cy(my).start()
    cz(z, yl, my, 0, zp).start()
    cz(z, yl, my, 1, zm).start()

    oz(z3, 0, zp).wait_recv()
    orl(z3, myq1, 0, zp).start()
    oy(z3, 1, my).start()
    oz(z1, 1, zm).wait_recv()
    orl(z1, myq2, 1, zm).start()
    oy(z1, 2, my).start()
    cy(his).wait_recv()
    cz(z, 1 - yl, his, 0, zp).start()
    cz(z, 1 - yl, his, 1, zm).start()

    xf[...] = jnp.zeros_like(xf)
    cf[...] = jnp.zeros_like(cf)

    def dd_copy(par, e, zc):
        rows = pl.ds(pl.multiple_of(zc * fc, fc), fc)
        return pltpu.make_async_copy(dd.at[par, e], dd_hbm.at[e, rows], dd_sem.at[par, e])

    def second(r, carry):
        off = 3 * r - 5 * (r // 2) - 2 * (r // 3)
        zc = (z + off) % NZ
        cols = pl.ds(pl.multiple_of(zc * fc, fc), fc)
        par = r % 2

        @pl.when(r == 0)
        def _():
            oy(z, 0, his).wait_recv()

        @pl.when(r == 1)
        def _():
            orl(z2, myq1, 0, zp).wait_recv()
            orl(z2, myq2, 1, zm).wait_recv()
            oy(z2, 3, my).start()
            cz(z3, 0, h1, 0, zp).wait_recv()
            crl(z3, h1, 0, zp).start()
            cz(z1, 1, h2, 1, zm).wait_recv()
            crl(z1, h2, 1, zm).start()
            cz(z3, 1, h2, 0, zp).wait_recv()
            oy(z3, 1, his).wait_recv()

        @pl.when(r == 2)
        def _():
            cz(z1, 0, h1, 1, zm).wait_recv()
            oy(z1, 2, his).wait_recv()

        @pl.when(r == 3)
        def _():
            crl(z2, h1, 0, zp).wait_recv()
            crl(z2, h2, 1, zm).wait_recv()
            oy(z2, 3, his).wait_recv()

        def expert(e, c2):
            is_c = (common == e).astype(F32)
            mc = is_c.astype(BF)
            hit = mo[e]
            hs = hc[zc, 0] * mc + ho[zc, 0] * hit
            dgs = hc[zc, 1] * mc + ho[zc, 1] * hit
            dus = hc[zc, 2] * mc + ho[zc, 2] * hit
            comb = cb[0] * is_c + cb[1] * (1.0 - is_c)

            @pl.when(r >= 2)
            def _():
                dd_copy(par, e, zc).wait()

            for i in range(nt):
                ns = pl.ds(i * 256, 256)
                xf[:, ns] += comb * mm(hs, wd[e, cols, ns])
                cf[:, ns] += mm_nt(dgs, wgu[0, e, ns, cols]) + mm_nt(dus, wgu[1, e, ns, cols])
                rgs = rgc[:, ns] * mc + rgo[:, ns] * (1.0 - is_c).astype(BF)
                dd[par, e, :, ns] = mm_tn(hs, rgs).astype(BF)
            dd_copy(par, e, zc).start()
            return c2

        lax.fori_loop(0, EXPERTS, expert, 0)
        return carry

    lax.fori_loop(0, NZ, second, 0)

    mine = pl.ds(pl.multiple_of(core * half, half), half)
    theirs = pl.ds(pl.multiple_of((1 - core) * half, half), half)
    fs[0] = xf[theirs, :].astype(BF)
    fs[1] = cf[theirs, :].astype(BF)
    pair = ten(fs, fr, f_send.at[0], f_recv.at[8], sib)
    pair.start()
    pair.wait_recv()
    xf[mine, :] += fr[0].astype(F32)
    cf[mine, :] += fr[1].astype(F32)

    def rows_of(k):
        return pl.ds(pl.multiple_of(core * half + k * bl, 8), bl)

    def both(k):
        return jnp.concatenate([xf[rows_of(k), :], cf[rows_of(k), :]], 0)

    def out_send(k):
        return ten(gs.at[k], gr.at[kt], f_send.at[k], f_recv.at[kt], k * 2 + core)

    def send(i, carry):
        k = (kt + i) % 8
        gs[k] = both(k).astype(BF)
        out_send(k).start()
        return carry

    pair.wait_send()
    lax.fori_loop(1, 8, send, 0)
    total = both(kt)
    for i in range(1, 8):
        k = (kt + i) % 8
        ten(gs.at[k], gr.at[k], f_send.at[k], f_recv.at[k], k * 2 + core).wait_recv()
        total += gr[k].astype(F32)
    lo_ref[...] = total[:bl].astype(BF)
    dt_ref[...] = total[bl:].astype(BF)

    for i in range(1, 8):
        out_send((kt + i) % 8).wait_send()
    for e in range(EXPERTS):
        dd_copy(0, e, z1).wait()
        dd_copy(1, e, z2).wait()
    for cp in own_sends + fwd_sends:
        cp.wait_send()
    for r in range(NZ):
        by(r).wait_send()
    for cp in (ar0, ar1, af0a, af0b, af1a, af1b, ay, br0, br1, bf0a, bf0b, bf1a, bf1b):
        cp.wait_send()
    oz(z, 0, zp).wait_send()
    oz(z, 1, zm).wait_send()
    orl(z3, myq1, 0, zp).wait_send()
    orl(z1, myq2, 1, zm).wait_send()
    for i, zc in enumerate((z, z3, z1, z2)):
        oy(zc, i, my).wait_send()
    cy(my).wait_send()
    for h, rows in ((yl, my), (1 - yl, his)):
        cz(z, h, rows, 0, zp).wait_send()
        cz(z, h, rows, 1, zm).wait_send()
    crl(z3, h1, 0, zp).wait_send()
    crl(z1, h2, 1, zm).wait_send()


def on_device(tokens, combine, expert_ids, expert_counts, w_gate, w_up, w_down, cotangent):
    total = combine.shape[0]
    bl, dloc = tokens.shape
    floc = w_gate.shape[2]
    fc = floc // NZ
    half, quart = total // 2, total // 4
    common = jnp.argmax(expert_counts == total).astype(jnp.int32)
    is_common = expert_ids == common
    comb_c = jnp.sum(jnp.where(is_common, combine, 0.0), 1)
    comb_o = jnp.sum(jnp.where(is_common, 0.0, combine), 1)
    other = jnp.sum(jnp.where(is_common, 0, expert_ids), 1).astype(F32)
    meta = jnp.stack([comb_c, comb_o, other, other], 1)
    meta = meta.reshape(8, 2, bl, 4).transpose(1, 0, 2, 3).reshape(total, 4)
    xt = jnp.concatenate([tokens, cotangent], 0)
    any_spec = pl.BlockSpec(memory_space=pl.ANY)
    vmem = pl.BlockSpec(memory_space=pltpu.VMEM)
    V = pltpu.VMEM
    dma = pltpu.SemaphoreType.DMA
    return pl.pallas_call(
        layer_kernel,
        out_shape=(
            jax.ShapeDtypeStruct((bl, dloc), BF),
            jax.ShapeDtypeStruct((bl, dloc), BF),
            jax.ShapeDtypeStruct((EXPERTS, floc, dloc), BF),
        ),
        in_specs=[pl.BlockSpec(memory_space=pltpu.SMEM), vmem, vmem, any_spec, any_spec, any_spec],
        out_specs=(vmem, vmem, any_spec),
        scratch_shapes=[
            V((2, EXPERTS, dloc, floc), BF),
            V((EXPERTS, floc, dloc), BF),
            V((16, 2 * bl, dloc), BF),
            V((total, dloc), F32),
            V((total, dloc), F32),
            V((total, dloc), BF),
            V((EXPERTS - 1, total, dloc), BF),
            V((total, dloc), BF),
            V((total, dloc), BF),
            V((EXPERTS - 1, total, dloc), BF),
            V((EXPERTS, total, fc), BF),
            V((2, total, 256), F32),
            V((NZ, 3, total, fc), BF),
            V((NZ, 3, total, fc), F32),
            V((NZ, 3, total, fc), BF),
            V((NZ, 3, total, fc), F32),
            V((2, 3, half, fc), BF),
            V((2, 3, total, fc), BF),
            V((3, half, fc), BF),
            V((3, half, fc), BF),
            V((NZ, 3, half, fc), BF),
            V((3, 3, half, fc), BF),
            V((2, 3, quart, fc), BF),
            V((2, 3, half, fc), BF),
            V((NZ, 3, total, fc), BF),
            V((NZ, 3, total, fc), BF),
            V((2, EXPERTS, fc, dloc), BF),
            V((2, half, dloc), BF),
            V((2, half, dloc), BF),
            V((8, 2 * bl, dloc), BF),
            V((8, 2 * bl, dloc), BF),
            dma((3, EXPERTS)),
            dma,
            dma((15,)),
            dma((16,)),
            dma((7,)),
            dma((7,)),
            dma((10,)),
            dma((10,)),
            dma((7,)),
            dma((7,)),
            dma((8,)),
            dma((8,)),
            dma((2, EXPERTS)),
            dma((8,)),
            dma((9,)),
        ],
        compiler_params=pltpu.CompilerParams(
            collective_id=0, has_side_effects=True, vmem_limit_bytes=67043328
        ),
    )(common.reshape(1), meta, xt, w_gate, w_up, w_down)


def solution(mesh):
    in_specs = (
        P("tensor", "section"),
        P(),
        P(),
        P(),
        P(None, "section", "tensor"),
        P(None, "section", "tensor"),
        P(None, "tensor", "section"),
        P("tensor", "section"),
    )
    out_specs = (P("tensor", "section"), P("tensor", "section"), P(None, "tensor", "section"))
    return jax.shard_map(
        on_device, mesh=mesh, in_specs=in_specs, out_specs=out_specs, check_vma=False
    )
```

time: 353 us -> 126 us (0.36)
  waiting for transfers between devices: 195 us -> 0 us
  Pallas kernels: 0 us -> 109 us
  blocking collectives: 58.2 us -> 0 us
  matrix products: 33.6 us -> 0 us
  between operations: 18.8 us -> 0.67 us
  local copies, waits for them, and re-layouts: 26.5 us -> 9.79 us
  other arithmetic: 18.6 us -> 5.45 us
    all_gather x2 -> x0, waiting for transfers between devices: 134 us -> none  [the longest x1 95.8 us: on_device(): full = lax.all_gather(mine, 'section', axis=0)]
    pallas_call x0 -> x1, Pallas kernels: none -> 109 us  [on_device(): pl.pallas_call(layer_kernel, out_shape=(jax.ShapeDtypeStruct((bl, dloc),...]
    reduce_scatter x1 -> x0, waiting for transfers between devices: 61.6 us -> none  [on_device(): lax.psum_scatter(jnp.stack([out, dtok]), 'tensor', scatter_dimension=1, t...]
    all_to_all x1 -> x0, blocking collectives: 58.2 us -> none  [on_device(): lax.all_to_all(parts, 'section', 0, 0, tiled=True).astype(jnp.float32)]
    dot_general x22 -> x0, matrix products: 33.6 us -> none  [dot(): lax.dot_general(a, b, (dims, ((), ())), preferred_element_type=jnp.float32)]
    another operation x5 -> x0, other arithmetic: 7.31 us -> none  [the longest x1 3.18 us: on_device(): return (res[0], res[1], jnp.stack(d_down))]
    select_n x4 -> x0, other arithmetic: 7.08 us -> none  [the longest x2 3.63 us: pick_all(): jnp.where(common == e, rows_c, jnp.where(mask_o[e], rows_o, jnp.zeros_lik...]
    all_gather x1 -> x0, local copies, waits for them, and re-layouts: 6.62 us -> none  [on_device(): full = lax.all_gather(mine, 'section', axis=0)]
  transfers between devices with their start and end apart: 3 -> 0, of which waited for: 3 -> 0; matrix products, arithmetic and copies ran while one was open for 6% -> 0% of each run, Pallas kernels for 0% -> 0%
where the time goes in v2:
time: 126 us; the launch traced here: 125 us
  Pallas kernels  109 us (87%)
  local copies, waits for them, and re-layouts  9.79 us (8%)
  other arithmetic  5.45 us (4%)
    pallas_call x1, Pallas kernels, on_device(): pl.pallas_call(layer_kernel, out_shape=(jax.ShapeDtypeStruct((bl, dloc),...  109 us
    unnamed x3, local copies, waits for them, and re-layouts  8.66 us

profile of v2, /device:TPU:1, one launch (start us, length us, event | category | flops | bytes accessed | tf_op | source)
XLA Modules:
  0.0 125.1 jit_solution(11834213642579024943)
XLA Ops:
  0.6 1.3 %compare_reduce_fusion = (pred[]{:T(512)}, s32[]{:T(128)}) fusion(s32[4]{0:T(128)} %param.11), kind=kLoop, calls=%fused_computation.5 | loop fusion | flops 25 | bytes 21 | tf_op jit(solution)/shard_map/on_device/reduce | solution.py:462
  1.9 1.3 %select_reduce_fusion = s32[384]{0:T(512)S(1)} fusion(s32[384,2]{0,1:T(2,128)} %param.10, s32[]{:T(128)} %get-tuple-element.4), kind=kLoop, calls=%fused_computation.2 | loop fusion | flops 1920 | bytes 4612 | tf_op jit(solution)/shard_map/reduce_sum | solution.py:466
  3.3 1.4 %select_reduce_fusion.2 = (f32[384]{0:T(512)S(1)}, f32[384]{0:T(512)S(1)}) fusion(f32[384,2]{0,1:T(2,128)} %param.9, s32[384,2]{0,1:T(2,128)} %param.10, s32[]{:T(128)} %get-tuple-element.4), kind=kLoop, calls=%fused_computation.4 | loop fusion | flops 3072 | bytes 9220 | tf_op jit(solution)/shard_map/reduce_sum | solution.py:464
  4.7 0.1 stack.11
  4.8 0.1 convert_element_type.16
  4.9 0.1 stack.12
  5.0 1.4 %pad_maximum_fusion.xt_ref = bf16[48,768]{1,0:T(8,128)(2,1)} fusion(bf16[24,768]{1,0:T(8,128)(2,1)} %param.15, bf16[24,768]{1,0:T(8,128)(2,1)} %param.8), kind=kLoop, calls=%fused_computation | loop fusion | flops 147456 | bytes 147456 | tf_op jit(solution)/shard_map/concatenate | solution.py:469
  6.4 0.8 copy.11
  7.2 109.2 %shard_map.103 = (bf16[24,768]{1,0:T(8,128)(2,1)}, bf16[24,768]{1,0:T(8,128)(2,1)}, bf16[4,1024,768]{2,1,0:T(8,128)(2,1)}) custom-call(s32[1]{0:T(128)} %bitcast.c_ref, f32[384,4]{1,0:T(8,128)} %bitcast.4, bf16[48,768]{1,0:T(8,128)(2,1)} %pad_maximum_fusion.xt_ref, bf16[4,768,1024]{2,1,0:T(8,128)(2,1)} %wg_hbm.1, bf16[4,768,1024]{2,1,0:T(8,128)(2,1)} %wu_hbm.1, ...), custom_call_target="tpu_custom_call" | custom-call | tf_op jit(solution)/shard_map/pallas_call | solution.py:474
  116.4 1.4 %copy.15 = bf16[24,768]{1,0:T(8,128)(2,1)} copy(bf16[24,768]{1,0:T(8,128)(2,1)} %get-tuple-element.10) | data formatting | bytes 73728
  117.8 1.4 %copy.16 = bf16[24,768]{1,0:T(8,128)(2,1)} copy(bf16[24,768]{1,0:T(8,128)(2,1)} %get-tuple-element.11) | data formatting | bytes 73728
  119.2 5.9 %copy.17 = bf16[4,1024,768]{2,1,0:T(8,128)(2,1)} copy(bf16[4,1024,768]{2,1,0:T(8,128)(2,1)} %get-tuple-element.12) | data formatting | bytes 12582912
  (2 shorter events, 0.0 us)

commit v3 on v1

v3 whole, which is shorter than its diff:
```python
import jax
import jax.numpy as jnp
from jax import lax
from jax.experimental import pallas as pl
from jax.experimental.pallas import tpu as pltpu
from jax.sharding import PartitionSpec as P

EXPERTS = 4
NZ = 4
VLIM = 60000000
BF = jnp.bfloat16
F32 = jnp.float32
MESH = pl.DeviceIdType.MESH


def mm(a, b):
    return jnp.dot(a, b, preferred_element_type=F32)


def mm_nt(a, b):
    return lax.dot_general(a, b, (((1,), (1,)), ((), ())), preferred_element_type=F32)


def mm_tn(a, b):
    return lax.dot_general(a, b, (((0,), (0,)), ((), ())), preferred_element_type=F32)


def layer_kernel(
    counts_ref, comb_ref, ids_ref, tok_ref, cot_ref, wg_hbm, wu_hbm, wd_hbm,
    lo_ref, dt_ref, dd_ref,
    wgu, wd, tbuf, cbuf, meta, xf, cf, xs, xm, rgc, rgo, rgm, mo, cb,
    pa, paf, pb, pbf, rar, raf, sa, ray, rby, qb, rbr, rbf, hc, ho, fs, fr, gs, gr,
    w_sem, loc_sem, x_send, x_recv, a_send, a_recv, b_send, b_recv,
    c_send, c_recv, o_send, o_recv, p_send, p_recv, f_send, f_recv,
):
    tokens, dloc = xf.shape
    fc = pa.shape[-1]
    half = tokens // 2
    quart = half // 2
    bl = tokens // 16
    nt = dloc // 256

    s = lax.axis_index("section")
    t = lax.axis_index("tensor")
    z, yl = s // 2, s % 2
    zp = ((z + 1) % NZ) * 2 + yl
    zm = ((z + 3) % NZ) * 2 + yl
    yp = z * 2 + 1 - yl
    zdev = (zp, zm)
    core, kt, x = t % 2, t // 2, t // 4
    yh = kt % 2

    def tx(d):
        return ((x + d) % 4) * 4 + yh * 2 + core

    ty = x * 4 + (1 - yh) * 2 + core
    sib = t + 1 - 2 * core

    def sec(src, dst, ssem, rsem, dev):
        return pltpu.make_async_remote_copy(src, dst, ssem, rsem, {"section": dev}, MESH)

    def ten(src, dst, ssem, rsem, dev):
        return pltpu.make_async_remote_copy(src, dst, ssem, rsem, {"tensor": dev}, MESH)

    def w_copy(a, e):
        if a == 2:
            return pltpu.make_async_copy(wd_hbm.at[e], wd.at[e], w_sem.at[2, e])
        return pltpu.make_async_copy((wg_hbm, wu_hbm)[a].at[e], wgu.at[a, e], w_sem.at[a, e])

    for a in range(3):
        for e in range(EXPERTS):
            w_copy(a, e).start()

    barrier = pltpu.get_barrier_semaphore()
    for dev in (zp, zm, yp):
        pl.semaphore_signal(barrier, inc=1, device_id={"section": dev}, device_id_type=MESH)
    for k in range(1, 8):
        pl.semaphore_signal(
            barrier, inc=1, device_id={"tensor": ((kt + k) % 8) * 2 + core}, device_id_type=MESH
        )
    pl.semaphore_signal(barrier, inc=1, device_id={"tensor": sib}, device_id_type=MESH)
    pl.semaphore_wait(barrier, 11)

    q = core * 8 + kt
    qy = core * 8 + x * 2 + 1 - yh
    targets = (ty, tx(1), tx(3), tx(2), sib)
    bufs = (tbuf, cbuf)
    srcs = (tok_ref, cot_ref)
    slots = [
        core * 8 + ((x + d) % 4) * 2 + yh + flip - 2 * yh * flip for flip in (0, 1) for d in (1, 3, 2)
    ]

    def own_copy(g):
        return pltpu.make_async_copy(srcs[g], bufs[g].at[q], loc_sem.at[g])

    def own_send(g, i):
        return ten(srcs[g], bufs[g].at[q], x_send.at[g, i], x_recv.at[g, q], targets[i])

    def pass_on(g, i, slot, dev):
        return ten(bufs[g].at[slot], bufs[g].at[slot], x_send.at[g, i], x_recv.at[g, slot], dev)

    def gather_start(g):
        own_copy(g).start()
        for i in range(5):
            own_send(g, i).start()

    def gather_mid(g):
        pass_on(g, 0, qy, sib).wait_recv()
        for i in range(4):
            pass_on(g, 5 + i, qy, targets[1 + i]).start()

    def gather_pair(g):
        for i in range(6):
            pass_on(g, 0, slots[i], sib).wait_recv()
            pass_on(g, 9 + i, slots[i], sib).start()

    def gather_end(g):
        for k in range(8):
            pass_on(g, 0, (1 - core) * 8 + k, sib).wait_recv()
        own_copy(g).wait()

    gather_start(0)

    common = jnp.int32(EXPERTS - 1)
    for e in range(EXPERTS - 2, -1, -1):
        common = jnp.where(counts_ref[e] == tokens, e, common)
    others = [(common + 1 + j) % EXPERTS for j in range(EXPERTS - 1)]
    ids, cmb = ids_ref[...], comb_ref[...]
    is_c = ids == common
    cc_row = jnp.sum(jnp.where(is_c, cmb, 0.0), 0, keepdims=True)
    co_row = jnp.sum(jnp.where(is_c, 0.0, cmb), 0, keepdims=True)
    id_row = jnp.sum(jnp.where(is_c, 0.0, ids.astype(F32)), 0, keepdims=True)
    which = lax.broadcasted_iota(jnp.int32, (128, tokens), 0)
    grid = jnp.where(which == 0, cc_row, jnp.where(which == 1, co_row, id_row))
    columns = grid.T
    for i in range(16):
        at = (i % 2) * 8 + i // 2
        meta[at * bl : (at + 1) * bl, :] = columns[i * bl : (i + 1) * bl, :]

    gather_mid(0)
    gather_pair(0)
    gather_end(0)
    gather_start(1)

    rt = 32

    def spread(buf, dst):
        def split(i, carry):
            dst[pl.ds(pl.multiple_of(i * bl, 8), bl), :] = buf[i].astype(F32)
            return carry

        lax.fori_loop(0, 16, split, 0)

    def prep_x(i, carry):
        rows = pl.ds(pl.multiple_of(i * rt, rt), rt)
        oid = meta[rows, 2:3]
        xv = xf[rows, :]
        xs[rows, :] = xv.astype(BF)
        for j, e in enumerate(others):
            xm[j, rows, :] = jnp.where(oid == e.astype(F32), xv, 0.0).astype(BF)
        return carry

    def prep_c(i, carry):
        rows = pl.ds(pl.multiple_of(i * rt, rt), rt)
        m = meta[rows, :]
        cc, co, oid = m[:, 0:1], m[:, 1:2], m[:, 2:3]
        cv = cf[rows, :]
        ro = (co * cv).astype(BF).astype(F32)
        rgc[rows, :] = (cc * cv).astype(BF)
        rgo[rows, :] = ro.astype(BF)
        for j, e in enumerate(others):
            rgm[j, rows, :] = jnp.where(oid == e.astype(F32), ro, 0.0).astype(BF)
        for e in range(EXPERTS):
            hit = (oid == float(e)).astype(F32)
            mo[e, rows, :] = jnp.broadcast_to(hit, (rt, fc)).astype(BF)
        cb[0, rows, :] = jnp.broadcast_to(cc, (rt, 256))
        cb[1, rows, :] = jnp.broadcast_to(co, (rt, 256))
        return carry

    spread(tbuf, xf)
    lax.fori_loop(0, tokens // rt, prep_x, 0)
    for a in range(2):
        for e in range(EXPERTS):
            w_copy(a, e).wait()

    my = pl.ds(pl.multiple_of(yl * half, half), half)
    his = pl.ds(pl.multiple_of((1 - yl) * half, half), half)
    hh = (pl.ds(0, half), pl.ds(half, half))
    qq = (pl.ds(0, quart), pl.ds(quart, quart))
    mq = (
        pl.ds(pl.multiple_of(yl * half, quart), quart),
        pl.ds(pl.multiple_of(yl * half + quart, quart), quart),
    )
    gg = (pl.ds(0, 2), pl.ds(2, 1))

    def by(g, r):
        return sec(pb.at[r, gg[g], his], rby.at[r, gg[g]], b_send.at[g, r], b_recv.at[g, r], yp)

    def ar(g, d):
        return sec(
            pa.at[0, gg[g], hh[d]], rar.at[d, gg[g]], a_send.at[g, d], a_recv.at[g, d], zdev[d]
        )

    def af(g, d, h):
        i = 2 + 2 * d + h
        return sec(
            pa.at[1 + d, gg[g], hh[h]], raf.at[d, gg[g], hh[h]], a_send.at[g, i], a_recv.at[g, i],
            zdev[d],
        )

    def ay(g):
        return sec(sa.at[gg[g]], ray.at[gg[g]], a_send.at[g, 6], a_recv.at[g, 6], yp)

    def br(g, d):
        i = 4 + d
        return sec(
            qb.at[0, gg[g], qq[d]], rbr.at[d, gg[g]], b_send.at[g, i], b_recv.at[g, i], zdev[d]
        )

    def bf(g, d, h):
        i = 6 + 2 * d + h
        return sec(
            qb.at[1 + d, gg[g], qq[h]], rbf.at[d, gg[g], qq[h]], b_send.at[g, i], b_recv.at[g, i],
            zdev[d],
        )

    def chunk_of(r):
        zc = (z + 2 - r + 3 * (r // 2) - 2 * (r // 3)) % NZ
        return pl.ds(pl.multiple_of(zc * fc, fc), fc)

    def leave(g, r):
        @pl.when(r == 0)
        def _():
            ar(g, 0).start()
            ar(g, 1).start()

        @pl.when(r == 1)
        def _():
            af(g, 0, 1).start()

        @pl.when(r == 2)
        def _():
            af(g, 1, 0).start()

    def first_gu(r, carry):
        cols = chunk_of(r)

        @pl.when(r == 2)
        def _():
            gather_mid(1)

        def proj_o(a, c2):
            acc = mm(xm[0], wgu[a, others[0], :, cols])
            acc += mm(xm[1], wgu[a, others[1], :, cols])
            acc += mm(xm[2], wgu[a, others[2], :, cols])
            pbf[r, a] = acc
            pb[r, a] = acc.astype(BF)
            return c2

        lax.fori_loop(0, 2, proj_o, 0)
        by(0, r).start()

        def proj_c(a, c2):
            acc = mm(xs[...], wgu[a, common, :, cols])
            paf[r, a] = acc
            pa[r, a] = acc.astype(BF)
            return c2

        lax.fori_loop(0, 2, proj_c, 0)
        leave(0, r)
        return carry

    def first_dh(r, carry):
        cols = chunk_of(r)
        acc = mm_nt(rgm[0], wd[others[0], cols, :])
        acc += mm_nt(rgm[1], wd[others[1], cols, :])
        acc += mm_nt(rgm[2], wd[others[2], cols, :])
        pbf[r, 2] = acc
        pb[r, 2] = acc.astype(BF)
        by(1, r).start()
        acc = mm_nt(rgc[...], wd[common, cols, :])
        paf[r, 2] = acc
        pa[r, 2] = acc.astype(BF)
        leave(1, r)
        return carry

    def a_relay(g):
        for d in (0, 1):
            ar(g, d).wait_recv()
            pa[1 + d, gg[g], hh[d]] = (
                paf[1 + d, gg[g], hh[d]] + rar[d, gg[g]].astype(F32)
            ).astype(BF)
            af(g, d, d).start()

    def a_final(g):
        for d in (0, 1):
            for h in (0, 1):
                af(g, d, h).wait_recv()
        sa[gg[g]] = (
            paf[3, gg[g], his]
            + raf[0, gg[g], his].astype(F32)
            + raf[1, gg[g], his].astype(F32)
        ).astype(BF)
        ay(g).start()

    def b_step(g, r):
        by(g, r).wait_recv()
        if r == 0:
            qb[0, gg[g]] = (pbf[0, gg[g], my] + rby[0, gg[g]].astype(F32)).astype(BF)
            br(g, 0).start()
            br(g, 1).start()
        elif r < 3:
            d = r - 1
            h = 1 - d
            qb[r, gg[g], qq[h]] = (
                pbf[r, gg[g], mq[h]] + rby[r, gg[g], qq[h]].astype(F32)
            ).astype(BF)
            bf(g, d, h).start()
            br(g, d).wait_recv()
            qb[r, gg[g], qq[d]] = (
                pbf[r, gg[g], mq[d]]
                + rby[r, gg[g], qq[d]].astype(F32)
                + rbr[d, gg[g]].astype(F32)
            ).astype(BF)
            bf(g, d, d).start()

    lax.fori_loop(0, NZ, first_gu, 0)
    gather_pair(1)
    a_relay(0)
    b_step(0, 0)
    gather_end(1)
    spread(cbuf, cf)
    lax.fori_loop(0, tokens // rt, prep_c, 0)
    for e in range(EXPERTS):
        w_copy(2, e).wait()
    lax.fori_loop(0, NZ, first_dh, 0)
    b_step(0, 1)
    a_relay(1)
    b_step(0, 2)
    a_final(0)
    b_step(0, 3)
    b_step(1, 0)
    b_step(1, 1)
    b_step(1, 2)
    a_final(1)
    b_step(1, 3)

    def swiglu(total, dst):
        gate, up, dh = total(0), total(1), total(2)
        sg = 1.0 / (1.0 + jnp.exp(-gate))
        act = gate * sg
        dst[z, 0, my, :] = (act * up).astype(BF)
        dst[z, 1, my, :] = (dh * up * sg * (1.0 + gate * (1.0 - sg))).astype(BF)
        dst[z, 2, my, :] = (dh * act).astype(BF)

    for g in (0, 1):
        for d in (0, 1):
            for h in (0, 1):
                bf(g, d, h).wait_recv()
    swiglu(
        lambda a: pbf[3, a, my, :]
        + rby[3, a].astype(F32)
        + rbf[0, a].astype(F32)
        + rbf[1, a].astype(F32),
        ho,
    )

    z1, z3, z2 = (z + 1) % NZ, (z + 3) % NZ, (z + 2) % NZ

    def oz(zc, d):
        return sec(ho.at[zc, :, my], ho.at[zc, :, my], o_send.at[d], o_recv.at[d], zdev[d])

    def oy(zc, i, rows):
        return sec(ho.at[zc, :, rows], ho.at[zc, :, rows], o_send.at[4 + i], o_recv.at[4 + i], yp)

    def orl(zc, d):
        part = ho.at[zc, :, mq[d]]
        return sec(part, part, o_send.at[2 + d], o_recv.at[2 + d], zdev[d])

    oz(z, 0).start()
    oz(z, 1).start()
    oy(z, 0, my).start()

    ay(0).wait_recv()
    ay(1).wait_recv()
    swiglu(
        lambda a: paf[3, a, my, :]
        + raf[0, a, my, :].astype(F32)
        + raf[1, a, my, :].astype(F32)
        + ray[a].astype(F32),
        hc,
    )

    def cy(rows):
        return sec(hc.at[z, :, rows], hc.at[z, :, rows], c_send.at[0], c_recv.at[0], yp)

    def cz(zc, h, rows, d):
        i = 1 + 2 * d + h
        return sec(hc.at[zc, :, rows], hc.at[zc, :, rows], c_send.at[i], c_recv.at[i], zdev[d])

    def crl(zc, d):
        part = hc.at[zc, :, hh[d]]
        return sec(part, part, c_send.at[5 + d], c_recv.at[5 + d], zdev[d])

    cy(my).start()
    cz(z, yl, my, 0).start()
    cz(z, yl, my, 1).start()

    oz(z3, 0).wait_recv()
    orl(z3, 0).start()
    oy(z3, 1, my).start()
    oz(z1, 1).wait_recv()
    orl(z1, 1).start()
    oy(z1, 2, my).start()
    cy(his).wait_recv()
    cz(z, 1 - yl, his, 0).start()
    cz(z, 1 - yl, his, 1).start()

    xf[...] = jnp.zeros_like(xf)
    cf[...] = jnp.zeros_like(cf)
    for g in (0, 1):
        for r in range(NZ):
            by(g, r).wait_send()

    mine = pl.ds(pl.multiple_of(core * half, half), half)
    theirs = pl.ds(pl.multiple_of((1 - core) * half, half), half)

    def tile(i):
        return pl.ds(pl.multiple_of(i * 256, 256), 256)

    def pair(i):
        return ten(fs.at[i], fr.at[i], p_send.at[i], p_recv.at[i], sib)

    def out_send(i, k):
        return ten(gs.at[i, k], gr.at[i, kt], f_send.at[i, k], f_recv.at[i, kt], k * 2 + core)

    def both(i, k):
        rows = pl.ds(pl.multiple_of(core * half + k * bl, 8), bl)
        return jnp.concatenate([xf[rows, tile(i)], cf[rows, tile(i)]], 0)

    def flush(i):
        pair(i).wait_recv()
        xf[mine, tile(i)] += fr[i, 0].astype(F32)
        cf[mine, tile(i)] += fr[i, 1].astype(F32)

        def send(n, carry):
            k = (kt + n) % 8
            gs[i, k] = both(i, k).astype(BF)
            out_send(i, k).start()
            return carry

        lax.fori_loop(1, 8, send, 0)

    def second(r, carry):
        zc = (z + 3 * r - 5 * (r // 2) - 2 * (r // 3)) % NZ
        cols = pl.ds(pl.multiple_of(zc * fc, fc), fc)

        @pl.when(r == 1)
        def _():
            for d in (0, 1):
                orl(z2, d).wait_recv()
            oy(z2, 3, my).start()
            cz(z3, 0, hh[0], 0).wait_recv()
            crl(z3, 0).start()
            cz(z1, 1, hh[1], 1).wait_recv()
            crl(z1, 1).start()
            cz(z3, 1, hh[1], 0).wait_recv()

        @pl.when(r == 2)
        def _():
            cz(z1, 0, hh[0], 1).wait_recv()

        @pl.when(r == 3)
        def _():
            crl(z2, 0).wait_recv()
            crl(z2, 1).wait_recv()

        def common_tile(i, c2):
            ns = tile(i)
            xf[:, ns] += cb[0] * mm(hc[zc, 0], wd[common, cols, ns])
            cf[:, ns] += mm_nt(hc[zc, 1], wgu[0, common, ns, cols]) + mm_nt(
                hc[zc, 2], wgu[1, common, ns, cols]
            )
            return c2

        lax.fori_loop(0, nt, common_tile, 0)

        @pl.when(r == 0)
        def _():
            oy(z, 0, his).wait_recv()

        @pl.when(r == 1)
        def _():
            oy(z3, 1, his).wait_recv()

        @pl.when(r == 2)
        def _():
            oy(z1, 2, his).wait_recv()

        @pl.when(r == 3)
        def _():
            oy(z2, 3, his).wait_recv()

        for j, e in enumerate(others):
            hit = mo[e]
            for a in range(3):
                pb[j, a] = ho[zc, a] * hit

        def other_tile(i, c2):
            ns = tile(i)
            acc = mm(pb[0, 0], wd[others[0], cols, ns])
            acc += mm(pb[1, 0], wd[others[1], cols, ns])
            acc += mm(pb[2, 0], wd[others[2], cols, ns])
            xf[:, ns] += cb[1] * acc
            acc = mm_nt(pb[0, 1], wgu[0, others[0], ns, cols])
            acc += mm_nt(pb[0, 2], wgu[1, others[0], ns, cols])
            for j in (1, 2):
                acc += mm_nt(pb[j, 1], wgu[0, others[j], ns, cols])
                acc += mm_nt(pb[j, 2], wgu[1, others[j], ns, cols])
            cf[:, ns] += acc

            @pl.when(r == 3)
            def _():
                fs[i, 0] = xf[theirs, ns].astype(BF)
                fs[i, 1] = cf[theirs, ns].astype(BF)
                pair(i).start()

                @pl.when(i > 0)
                def _():
                    flush(i - 1)

            return c2

        lax.fori_loop(0, nt, other_tile, 0)
        return carry

    lax.fori_loop(0, NZ, second, 0)
    flush(nt - 1)

    def weight_grad(e, carry):
        here = (common == e).astype(F32)
        mc = here.astype(BF)
        hit = mo[e]
        xs[...] = rgc[...] * mc + rgo[...] * (1.0 - here).astype(BF)

        def block(zc, c2):
            hs = hc[zc, 0] * mc + ho[zc, 0] * hit
            rows = pl.ds(pl.multiple_of(zc * fc, fc), fc)
            for i in range(nt):
                ns = pl.ds(i * 256, 256)
                dd_ref[e, rows, ns] = mm_tn(hs, xs[:, ns]).astype(BF)
            return c2

        lax.fori_loop(0, NZ, block, 0)
        return carry

    lax.fori_loop(0, EXPERTS, weight_grad, 0)

    for i in range(nt):
        total = both(i, kt)
        for n in range(1, 8):
            k = (kt + n) % 8
            dev = k * 2 + core
            ten(gs.at[i, k], gr.at[i, k], f_send.at[i, k], f_recv.at[i, k], dev).wait_recv()
            total += gr[i, k].astype(F32)
        lo_ref[:, i * 256 : (i + 1) * 256] = total[:bl].astype(BF)
        dt_ref[:, i * 256 : (i + 1) * 256] = total[bl:].astype(BF)

    for i in range(nt):
        pair(i).wait_send()
        for n in range(1, 8):
            out_send(i, (kt + n) % 8).wait_send()
    for g in (0, 1):
        for i in range(5):
            own_send(g, i).wait_send()
        for i in range(4):
            pass_on(g, 5 + i, qy, targets[1 + i]).wait_send()
        for i in range(6):
            pass_on(g, 9 + i, slots[i], sib).wait_send()
        for d in (0, 1):
            ar(g, d).wait_send()
            br(g, d).wait_send()
            for h in (0, 1):
                af(g, d, h).wait_send()
                bf(g, d, h).wait_send()
        ay(g).wait_send()
    for d, zc in ((0, z3), (1, z1)):
        oz(z, d).wait_send()
        orl(zc, d).wait_send()
        crl(zc, d).wait_send()
        cz(z, yl, my, d).wait_send()
        cz(z, 1 - yl, his, d).wait_send()
    for i, zc in enumerate((z, z3, z1, z2)):
        oy(zc, i, my).wait_send()
    cy(my).wait_send()


def on_device(tokens, combine, expert_ids, expert_counts, w_gate, w_up, w_down, cotangent):
    total = combine.shape[0]
    bl, dloc = tokens.shape
    floc = w_gate.shape[2]
    fc = floc // NZ
    half, quart = total // 2, total // 4
    nt = dloc // 256
    any_spec = pl.BlockSpec(memory_space=pl.ANY)
    vmem = pl.BlockSpec(memory_space=pltpu.VMEM)
    V = pltpu.VMEM
    dma = pltpu.SemaphoreType.DMA
    return pl.pallas_call(
        layer_kernel,
        out_shape=(V((bl, dloc), BF), V((bl, dloc), BF), V((EXPERTS, floc, dloc), BF)),
        in_specs=[pl.BlockSpec(memory_space=pltpu.SMEM)] + [vmem] * 4 + [any_spec] * 3,
        out_specs=(vmem, vmem, vmem),
        scratch_shapes=[
            V((2, EXPERTS, dloc, floc), BF),
            V((EXPERTS, floc, dloc), BF),
            V((16, bl, dloc), BF),
            V((16, bl, dloc), BF),
            V((total, 128), F32),
            V((total, dloc), F32),
            V((total, dloc), F32),
            V((total, dloc), BF),
            V((EXPERTS - 1, total, dloc), BF),
            V((total, dloc), BF),
            V((total, dloc), BF),
            V((EXPERTS - 1, total, dloc), BF),
            V((EXPERTS, total, fc), BF),
            V((2, total, 256), F32),
            V((NZ, 3, total, fc), BF),
            V((NZ, 3, total, fc), F32),
            V((NZ, 3, total, fc), BF),
            V((NZ, 3, total, fc), F32),
            V((2, 3, half, fc), BF),
            V((2, 3, total, fc), BF),
            V((3, half, fc), BF),
            V((3, half, fc), BF),
            V((NZ, 3, half, fc), BF),
            V((3, 3, half, fc), BF),
            V((2, 3, quart, fc), BF),
            V((2, 3, half, fc), BF),
            V((NZ, 3, total, fc), BF),
            V((NZ, 3, total, fc), BF),
            V((nt, 2, half, 256), BF),
            V((nt, 2, half, 256), BF),
            V((nt, 8, 2 * bl, 256), BF),
            V((nt, 8, 2 * bl, 256), BF),
            dma((3, EXPERTS)),
            dma((2,)),
            dma((2, 15)),
            dma((2, 16)),
            dma((2, 7)),
            dma((2, 7)),
            dma((2, 10)),
            dma((2, 10)),
            dma((7,)),
            dma((7,)),
            dma((8,)),
            dma((8,)),
            dma((nt,)),
            dma((nt,)),
            dma((nt, 8)),
            dma((nt, 8)),
        ],
        compiler_params=pltpu.CompilerParams(
            collective_id=0, has_side_effects=True, vmem_limit_bytes=VLIM
        ),
    )(expert_counts, combine.T, expert_ids.T, tokens, cotangent, w_gate, w_up, w_down)


def solution(mesh):
    in_specs = (
        P("tensor", "section"),
        P(),
        P(),
        P(),
        P(None, "section", "tensor"),
        P(None, "section", "tensor"),
        P(None, "tensor", "section"),
        P("tensor", "section"),
    )
    out_specs = (P("tensor", "section"), P("tensor", "section"), P(None, "tensor", "section"))
    return jax.shard_map(
        on_device, mesh=mesh, in_specs=in_specs, out_specs=out_specs, check_vma=False
    )
```

time: 353 us -> 107 us (0.30)
  waiting for transfers between devices: 195 us -> 0 us
  Pallas kernels: 0 us -> 102 us
  blocking collectives: 58.2 us -> 0 us
  matrix products: 33.6 us -> 0 us
  local copies, waits for them, and re-layouts: 26.5 us -> 3.94 us
  other arithmetic: 18.6 us -> 0 us
  between operations: 18.8 us -> 0.64 us
    all_gather x2 -> x0, waiting for transfers between devices: 134 us -> none  [the longest x1 95.8 us: on_device(): full = lax.all_gather(mine, 'section', axis=0)]
    pallas_call x0 -> x1, Pallas kernels: none -> 102 us  [on_device(): pl.pallas_call(layer_kernel, out_shape=(V((bl, dloc), BF), V((bl, dloc),...]
    reduce_scatter x1 -> x0, waiting for transfers between devices: 61.6 us -> none  [on_device(): lax.psum_scatter(jnp.stack([out, dtok]), 'tensor', scatter_dimension=1, t...]
    all_to_all x1 -> x0, blocking collectives: 58.2 us -> none  [on_device(): lax.all_to_all(parts, 'section', 0, 0, tiled=True).astype(jnp.float32)]
    dot_general x22 -> x0, matrix products: 33.6 us -> none  [dot(): lax.dot_general(a, b, (dims, ((), ())), preferred_element_type=jnp.float32)]
    another operation x6 -> x0, other arithmetic: 8.62 us -> none  [the longest x1 3.18 us: on_device(): return (res[0], res[1], jnp.stack(d_down))]
    select_n x4 -> x0, other arithmetic: 7.08 us -> none  [the longest x2 3.63 us: pick_all(): jnp.where(common == e, rows_c, jnp.where(mask_o[e], rows_o, jnp.zeros_lik...]
    all_gather x1 -> x0, local copies, waits for them, and re-layouts: 6.62 us -> none  [on_device(): full = lax.all_gather(mine, 'section', axis=0)]
  transfers between devices with their start and end apart: 3 -> 0, of which waited for: 3 -> 0; matrix products, arithmetic and copies ran while one was open for 6% -> 0% of each run, Pallas kernels for 0% -> 0%
where the time goes in v3:
time: 107 us
  Pallas kernels  102 us (95%)
  local copies, waits for them, and re-layouts  3.94 us (4%)
    pallas_call x1, Pallas kernels, on_device(): pl.pallas_call(layer_kernel, out_shape=(V((bl, dloc), BF), V((bl, dloc),...  102 us
    unnamed x3, local copies, waits for them, and re-layouts  3.94 us

profile of v3, /device:TPU:1, one launch (start us, length us, event | category | flops | bytes accessed | tf_op | source)
XLA Modules:
  0.0 106.6 jit_solution(17579641363773696402)
XLA Ops:
  0.6 102.0 %shard_map.103 = (bf16[24,768]{1,0:T(8,128)(2,1)S(1)}, bf16[24,768]{1,0:T(8,128)(2,1)S(1)}, bf16[4,1024,768]{2,1,0:T(8,128)(2,1)S(1)}) custom-call(s32[4]{0:T(128)} %counts_ref.1, f32[2,384]{1,0:T(2,128)} %bitcast.2, s32[2,384]{1,0:T(2,128)} %bitcast.3, bf16[24,768]{1,0:T(8,128)(2,1)} %tok_ref.1, bf16[24,768]{1,0:T(8,128)(2,1)} %cot_ref.1, ...), custom_call_target="tpu_custom_call" | custom-call | tf_op jit(solution)/shard_map/pallas_call | solution.py:609
  102.6 0.6 copy.14
  103.3 0.6 copy.15
  103.9 2.7 %copy.16 = bf16[4,1024,768]{2,1,0:T(8,128)(2,1)} copy(bf16[4,1024,768]{2,1,0:T(8,128)(2,1)S(1)} %get-tuple-element.5) | data formatting | bytes 12582912

commit v4 on v3

--- a/solution.py
+++ b/solution.py
@@ -8,6 +8,8 @@
 EXPERTS = 4
 NZ = 4
 VLIM = 60000000
+HOPS = ((2, 1), (1, 1), (3, 1), (0, 1), (2, 0), (1, 0), (3, 0))
+ORDER = (5, 6, 4, 3, 1, 2, 0)
 BF = jnp.bfloat16
 F32 = jnp.float32
 MESH = pl.DeviceIdType.MESH
@@ -82,13 +84,11 @@
     pl.semaphore_wait(barrier, 11)
 
     q = core * 8 + kt
-    qy = core * 8 + x * 2 + 1 - yh
-    targets = (ty, tx(1), tx(3), tx(2), sib)
     bufs = (tbuf, cbuf)
     srcs = (tok_ref, cot_ref)
-    slots = [
-        core * 8 + ((x + d) % 4) * 2 + yh + flip - 2 * yh * flip for flip in (0, 1) for d in (1, 3, 2)
-    ]
+    far = [((x + d) % 4) * 2 + yh + flip - 2 * yh * flip for d, flip in HOPS]
+    slots = [core * 8 + k for k in far]
+    targets = [k * 2 + core for k in far] + [sib]
 
     def own_copy(g):
         return pltpu.make_async_copy(srcs[g], bufs[g].at[q], loc_sem.at[g])
@@ -101,18 +101,13 @@
 
     def gather_start(g):
         own_copy(g).start()
-        for i in range(5):
+        for i in range(8):
             own_send(g, i).start()
 
-    def gather_mid(g):
-        pass_on(g, 0, qy, sib).wait_recv()
-        for i in range(4):
-            pass_on(g, 5 + i, qy, targets[1 + i]).start()
-
     def gather_pair(g):
-        for i in range(6):
+        for i in ORDER:
             pass_on(g, 0, slots[i], sib).wait_recv()
-            pass_on(g, 9 + i, slots[i], sib).start()
+            pass_on(g, 8 + i, slots[i], sib).start()
 
     def gather_end(g):
         for k in range(8):
@@ -137,34 +132,27 @@
         at = (i % 2) * 8 + i // 2
         meta[at * bl : (at + 1) * bl, :] = columns[i * bl : (i + 1) * bl, :]
 
-    gather_mid(0)
     gather_pair(0)
     gather_end(0)
     gather_start(1)
 
-    rt = 32
-
-    def spread(buf, dst):
-        def split(i, carry):
-            dst[pl.ds(pl.multiple_of(i * bl, 8), bl), :] = buf[i].astype(F32)
-            return carry
-
-        lax.fori_loop(0, 16, split, 0)
+    def pair_rows(buf, i):
+        return jnp.concatenate([buf[2 * i].astype(F32), buf[2 * i + 1].astype(F32)], 0)
 
     def prep_x(i, carry):
-        rows = pl.ds(pl.multiple_of(i * rt, rt), rt)
+        rows = pl.ds(pl.multiple_of(i * 2 * bl, 2 * bl), 2 * bl)
         oid = meta[rows, 2:3]
-        xv = xf[rows, :]
+        xv = pair_rows(tbuf, i)
         xs[rows, :] = xv.astype(BF)
         for j, e in enumerate(others):
             xm[j, rows, :] = jnp.where(oid == e.astype(F32), xv, 0.0).astype(BF)
         return carry
 
     def prep_c(i, carry):
-        rows = pl.ds(pl.multiple_of(i * rt, rt), rt)
+        rows = pl.ds(pl.multiple_of(i * 2 * bl, 2 * bl), 2 * bl)
         m = meta[rows, :]
         cc, co, oid = m[:, 0:1], m[:, 1:2], m[:, 2:3]
-        cv = cf[rows, :]
+        cv = pair_rows(cbuf, i)
         ro = (co * cv).astype(BF).astype(F32)
         rgc[rows, :] = (cc * cv).astype(BF)
         rgo[rows, :] = ro.astype(BF)
@@ -172,13 +160,12 @@
             rgm[j, rows, :] = jnp.where(oid == e.astype(F32), ro, 0.0).astype(BF)
         for e in range(EXPERTS):
             hit = (oid == float(e)).astype(F32)
-            mo[e, rows, :] = jnp.broadcast_to(hit, (rt, fc)).astype(BF)
-        cb[0, rows, :] = jnp.broadcast_to(cc, (rt, 256))
-        cb[1, rows, :] = jnp.broadcast_to(co, (rt, 256))
+            mo[e, rows, :] = jnp.broadcast_to(hit, (2 * bl, fc)).astype(BF)
+        cb[0, rows, :] = jnp.broadcast_to(cc, (2 * bl, 256))
+        cb[1, rows, :] = jnp.broadcast_to(co, (2 * bl, 256))
         return carry
 
-    spread(tbuf, xf)
-    lax.fori_loop(0, tokens // rt, prep_x, 0)
+    lax.fori_loop(0, 8, prep_x, 0)
     for a in range(2):
         for e in range(EXPERTS):
             w_copy(a, e).wait()
@@ -245,9 +232,14 @@
     def first_gu(r, carry):
         cols = chunk_of(r)
 
-        @pl.when(r == 2)
-        def _():
-            gather_mid(1)
+        def proj_c(a, c2):
+            acc = mm(xs[...], wgu[a, common, :, cols])
+            paf[r, a] = acc
+            pa[r, a] = acc.astype(BF)
+            return c2
+
+        lax.fori_loop(0, 2, proj_c, 0)
+        leave(0, r)
 
         def proj_o(a, c2):
             acc = mm(xm[0], wgu[a, others[0], :, cols])
@@ -259,29 +251,20 @@
 
         lax.fori_loop(0, 2, proj_o, 0)
         by(0, r).start()
-
-        def proj_c(a, c2):
-            acc = mm(xs[...], wgu[a, common, :, cols])
-            paf[r, a] = acc
-            pa[r, a] = acc.astype(BF)
-            return c2
-
-        lax.fori_loop(0, 2, proj_c, 0)
-        leave(0, r)
         return carry
 
     def first_dh(r, carry):
         cols = chunk_of(r)
+        acc = mm_nt(rgc[...], wd[common, cols, :])
+        paf[r, 2] = acc
+        pa[r, 2] = acc.astype(BF)
+        leave(1, r)
         acc = mm_nt(rgm[0], wd[others[0], cols, :])
         acc += mm_nt(rgm[1], wd[others[1], cols, :])
         acc += mm_nt(rgm[2], wd[others[2], cols, :])
         pbf[r, 2] = acc
         pb[r, 2] = acc.astype(BF)
         by(1, r).start()
-        acc = mm_nt(rgc[...], wd[common, cols, :])
-        paf[r, 2] = acc
-        pa[r, 2] = acc.astype(BF)
-        leave(1, r)
         return carry
 
     def a_relay(g):
@@ -329,20 +312,19 @@
     a_relay(0)
     b_step(0, 0)
     gather_end(1)
-    spread(cbuf, cf)
-    lax.fori_loop(0, tokens // rt, prep_c, 0)
+    lax.fori_loop(0, 8, prep_c, 0)
     for e in range(EXPERTS):
         w_copy(2, e).wait()
     lax.fori_loop(0, NZ, first_dh, 0)
     b_step(0, 1)
+    b_step(0, 2)
     a_relay(1)
-    b_step(0, 2)
     a_final(0)
     b_step(0, 3)
     b_step(1, 0)
     b_step(1, 1)
+    a_final(1)
     b_step(1, 2)
-    a_final(1)
     b_step(1, 3)
 
     def swiglu(total, dst):
@@ -443,13 +425,10 @@
         xf[mine, tile(i)] += fr[i, 0].astype(F32)
         cf[mine, tile(i)] += fr[i, 1].astype(F32)
 
-        def send(n, carry):
-            k = (kt + n) % 8
+        for d, flip in HOPS:
+            k = ((x + d) % 4) * 2 + yh + flip - 2 * yh * flip
             gs[i, k] = both(i, k).astype(BF)
             out_send(i, k).start()
-            return carry
-
-        lax.fori_loop(1, 8, send, 0)
 
     def second(r, carry):
         zc = (z + 3 * r - 5 * (r // 2) - 2 * (r // 3)) % NZ
@@ -571,12 +550,10 @@
         for n in range(1, 8):
             out_send(i, (kt + n) % 8).wait_send()
     for g in (0, 1):
-        for i in range(5):
+        for i in range(8):
             own_send(g, i).wait_send()
-        for i in range(4):
-            pass_on(g, 5 + i, qy, targets[1 + i]).wait_send()
-        for i in range(6):
-            pass_on(g, 9 + i, slots[i], sib).wait_send()
+        for i in range(7):
+            pass_on(g, 8 + i, slots[i], sib).wait_send()
         for d in (0, 1):
             ar(g, d).wait_send()
             br(g, d).wait_send()

time: 107 us -> 102 us (0.953)
  Pallas kernels: 102 us -> 97.2 us
    pallas_call x1, Pallas kernels: 102 us -> 97.2 us  [on_device(): pl.pallas_call(layer_kernel, out_shape=(V((bl, dloc), BF), V((bl, dloc),...]
where the time goes in v4:
time: 102 us
  Pallas kernels  97.2 us (95%)
  local copies, waits for them, and re-layouts  3.94 us (4%)
    pallas_call x1, Pallas kernels, on_device(): pl.pallas_call(layer_kernel, out_shape=(V((bl, dloc), BF), V((bl, dloc),...  97.2 us
    unnamed x3, local copies, waits for them, and re-layouts  3.94 us

profile of v4, /device:TPU:1, one launch (start us, length us, event | category | flops | bytes accessed | tf_op | source)
XLA Modules:
  0.0 101.8 jit_solution(6747433098880826430)
XLA Ops:
  0.6 97.2 %shard_map.103 = (bf16[24,768]{1,0:T(8,128)(2,1)S(1)}, bf16[24,768]{1,0:T(8,128)(2,1)S(1)}, bf16[4,1024,768]{2,1,0:T(8,128)(2,1)S(1)}) custom-call(s32[4]{0:T(128)} %counts_ref.1, f32[2,384]{1,0:T(2,128)} %bitcast.2, s32[2,384]{1,0:T(2,128)} %bitcast.3, bf16[24,768]{1,0:T(8,128)(2,1)} %tok_ref.1, bf16[24,768]{1,0:T(8,128)(2,1)} %cot_ref.1, ...), custom_call_target="tpu_custom_call" | custom-call | tf_op jit(solution)/shard_map/pallas_call | solution.py:586
  97.9 0.6 copy.14
  98.5 0.6 copy.15
  99.1 2.7 %copy.16 = bf16[4,1024,768]{2,1,0:T(8,128)(2,1)} copy(bf16[4,1024,768]{2,1,0:T(8,128)(2,1)S(1)} %get-tuple-element.5) | data formatting | bytes 12582912

commit v5 on v4

--- a/solution.py
+++ b/solution.py
@@ -255,6 +255,11 @@
 
     def first_dh(r, carry):
         cols = chunk_of(r)
+
+        @pl.when(r == 2)
+        def _():
+            b_step(0, 1)
+
         acc = mm_nt(rgc[...], wd[common, cols, :])
         paf[r, 2] = acc
         pa[r, 2] = acc.astype(BF)
@@ -316,7 +321,6 @@
     for e in range(EXPERTS):
         w_copy(2, e).wait()
     lax.fori_loop(0, NZ, first_dh, 0)
-    b_step(0, 1)
     b_step(0, 2)
     a_relay(1)
     a_final(0)
@@ -504,17 +508,14 @@
                 fs[i, 1] = cf[theirs, ns].astype(BF)
                 pair(i).start()
 
-                @pl.when(i > 0)
-                def _():
-                    flush(i - 1)
-
             return c2
 
         lax.fori_loop(0, nt, other_tile, 0)
         return carry
 
     lax.fori_loop(0, NZ, second, 0)
-    flush(nt - 1)
+    for i in range(nt):
+        flush(i)
 
     def weight_grad(e, carry):
         here = (common == e).astype(F32)

time: 102 us -> 102 us (level)
  no operation moved by 1% of the time
where the time goes in v5:
time: 102 us; the launch traced here: 101 us
  Pallas kernels  96.6 us (95%)
  local copies, waits for them, and re-layouts  3.94 us (4%)
    pallas_call x1, Pallas kernels, on_device(): pl.pallas_call(layer_kernel, out_shape=(V((bl, dloc), BF), V((bl, dloc),...  96.6 us
    unnamed x3, local copies, waits for them, and re-layouts  3.94 us

profile of v5, /device:TPU:1, one launch (start us, length us, event | category | flops | bytes accessed | tf_op | source)
XLA Modules:
  0.0 101.2 jit_solution(16876345889830832238)
XLA Ops:
  0.6 96.6 %shard_map.103 = (bf16[24,768]{1,0:T(8,128)(2,1)S(1)}, bf16[24,768]{1,0:T(8,128)(2,1)S(1)}, bf16[4,1024,768]{2,1,0:T(8,128)(2,1)S(1)}) custom-call(s32[4]{0:T(128)} %counts_ref.1, f32[2,384]{1,0:T(2,128)} %bitcast.2, s32[2,384]{1,0:T(2,128)} %bitcast.3, bf16[24,768]{1,0:T(8,128)(2,1)} %tok_ref.1, bf16[24,768]{1,0:T(8,128)(2,1)} %cot_ref.1, ...), custom_call_target="tpu_custom_call" | custom-call | tf_op jit(solution)/shard_map/pallas_call | solution.py:587
  97.2 0.6 copy.14
  97.9 0.6 copy.15
  98.5 2.7 %copy.16 = bf16[4,1024,768]{2,1,0:T(8,128)(2,1)} copy(bf16[4,1024,768]{2,1,0:T(8,128)(2,1)S(1)} %get-tuple-element.5) | data formatting | bytes 12582912

commit v6 on v5

--- a/solution.py
+++ b/solution.py
@@ -101,11 +101,17 @@
 
     def gather_start(g):
         own_copy(g).start()
-        for i in range(8):
+        for i in range(8) if g == 0 else (3, 4, 5, 6, 7):
             own_send(g, i).start()
 
+    def gather_mid():
+        pass_on(1, 0, slots[3], sib).wait_recv()
+        for i in range(3):
+            pass_on(1, i, slots[3], targets[4 + i]).start()
+        pass_on(1, 8 + 3, slots[3], sib).start()
+
     def gather_pair(g):
-        for i in ORDER:
+        for i in ORDER if g == 0 else (5, 6, 4, 1, 2, 0):
             pass_on(g, 0, slots[i], sib).wait_recv()
             pass_on(g, 8 + i, slots[i], sib).start()
 
@@ -231,6 +237,10 @@
 
     def first_gu(r, carry):
         cols = chunk_of(r)
+
+        @pl.when(r == 2)
+        def _():
+            gather_mid()
 
         def proj_c(a, c2):
             acc = mm(xs[...], wgu[a, common, :, cols])
@@ -552,7 +562,10 @@
             out_send(i, (kt + n) % 8).wait_send()
     for g in (0, 1):
         for i in range(8):
-            own_send(g, i).wait_send()
+            if g == 0 or i > 2:
+                own_send(g, i).wait_send()
+            else:
+                pass_on(g, i, slots[3], targets[4 + i]).wait_send()
         for i in range(7):
             pass_on(g, 8 + i, slots[i], sib).wait_send()
         for d in (0, 1):

time: 102 us -> 102 us (level)
  no operation moved by 1% of the time
where the time goes in v6:
time: 102 us
  Pallas kernels  97.1 us (95%)
  local copies, waits for them, and re-layouts  3.94 us (4%)
    pallas_call x1, Pallas kernels, on_device(): pl.pallas_call(layer_kernel, out_shape=(V((bl, dloc), BF), V((bl, dloc),...  97.1 us
    unnamed x3, local copies, waits for them, and re-layouts  3.94 us

profile of v6, /device:TPU:1, one launch (start us, length us, event | category | flops | bytes accessed | tf_op | source)
XLA Modules:
  0.0 101.7 jit_solution(3947663836580544538)
XLA Ops:
  0.6 97.1 %shard_map.103 = (bf16[24,768]{1,0:T(8,128)(2,1)S(1)}, bf16[24,768]{1,0:T(8,128)(2,1)S(1)}, bf16[4,1024,768]{2,1,0:T(8,128)(2,1)S(1)}) custom-call(s32[4]{0:T(128)} %counts_ref.1, f32[2,384]{1,0:T(2,128)} %bitcast.2, s32[2,384]{1,0:T(2,128)} %bitcast.3, bf16[24,768]{1,0:T(8,128)(2,1)} %tok_ref.1, bf16[24,768]{1,0:T(8,128)(2,1)} %cot_ref.1, ...), custom_call_target="tpu_custom_call" | custom-call | tf_op jit(solution)/shard_map/pallas_call | solution.py:600
  97.7 0.6 copy.14
  98.3 0.6 copy.15
  99.0 2.7 %copy.16 = bf16[4,1024,768]{2,1,0:T(8,128)(2,1)} copy(bf16[4,1024,768]{2,1,0:T(8,128)(2,1)S(1)} %get-tuple-element.5) | data formatting | bytes 12582912
